TPU v7x, 512 devices: a whole 4x4x16 slice. The times are simulated.
512 devices in a mesh: gx: 32 (over z, core), gy: 16 (over y, x).
Axes of the slice: x: 4, y: 4, z: 16, core: 2. Of those that a mesh axis runs over, the one named last changes fastest.
Arguments:
- operator: float32 [32, 16, 768, 768], P('gx', 'gy'), may hold values from -2 to 3, as said below
- loads: float32 [32, 16, 256, 768], P('gx', 'gy'), may hold values from -80 to 80
- warm: float32 [32, 16, 256, 768], P('gx', 'gy'), may hold values from -6 to 6
- orders: int32 [32, 16], replicated, may hold values from 256 to 768, as said below
- face_x: int32 [32, 16, 128], P('gx', 'gy'), may hold values from 0 to 767, as said below
- face_y: int32 [32, 16, 128], P('gx', 'gy'), may hold values from 0 to 767, as said below
- contact: int32 [32, 16, 768], P('gx', 'gy'), may hold values 0 or 1
Outputs:
- multipliers: float32 [32, 16, 256, 768], P('gx', 'gy')
Inputs may be any that keep to these rules, and one draw needn't show every extreme that they name: `orders`: multiples of 128; every draw has a subdomain of order 768; the orders of subdomains [i, j] and [(i + 16) mod 32, j] add up to 1024. `face_x`: 128 distinct rows of the subdomain, each below its order. `face_y`: 128 distinct rows of the subdomain, each below its order. `operator`: each matrix has a positive diagonal of order one.
All inputs are finite; a program needn't handle non-finite values. No bound on the sum of `contact` on one device may be relied on, other than what follows from the above.
Results may differ from a plain program's by a relative error of at most 0.00018.
Values sent between devices are 32-bit elements; how exact they have to be, the bound alone decides.
No kernel may reach another device: no remote copies, remote signals or barrier semaphores. Data moves between devices by JAX's collectives and lax.ppermute only.
A program may use at most 64 MiB of HBM per device.

v0:
```python
import jax
import jax.numpy as jnp
from jax import lax
from jax.sharding import Mesh
from jax.sharding import PartitionSpec as P

ORDER = 768
STRIP = 128
STRIPS = 6
ITERS = 3
GX = ("gx_0", "gx_1")
GY = ("gy_0", "gy_1")


step_length = 0.5
epsilon = 1e-06


def passed_along(block, axis, distance):
    devices = range(lax.axis_size(axis))
    route = [(i - distance, i) for i in devices if i - distance in devices]
    return lax.ppermute(block, axis, route)


def from_everyone(x, axis):
    copies = jnp.broadcast_to(x, (lax.axis_size(axis), *x.shape))
    return lax.all_to_all(copies, axis, split_axis=0, concat_axis=0, tiled=True)


def of_everyone(x, axis):
    everything = from_everyone(x, axis)
    return jnp.sum(everything, axis=0)


def over_axes(x, axes):
    far, near = axes
    nearer = of_everyone(x, near)
    return of_everyone(nearer, far)


def strip_product(multipliers, strip_rows):
    return lax.dot_general(
        multipliers,
        strip_rows,
        (((1,), (1,)), ((), ())),
        precision=lax.Precision.HIGHEST,
        preferred_element_type=jnp.float32,
    )


def strip_or_zero(active, multipliers, strip_rows):
    return lax.cond(
        active,
        lambda operands: strip_product(operands[0], operands[1]),
        lambda operands: jnp.zeros((operands[0].shape[0], operands[1].shape[0]), jnp.float32),
        (multipliers, strip_rows),
    )


def shift_columns(buffer, offset):
    return passed_along(buffer, GX, offset)


def shift_rows(buffer, offset):
    return passed_along(buffer, GY, offset)


def body(operator, loads, warm, orders, face_x, face_y, contact):
    operator_block = operator[0, 0]
    rows_x = face_x[0, 0]
    rows_y = face_y[0, 0]
    contact_here = contact[0, 0]
    count_x = lax.axis_size(GX)
    count_y = lax.axis_size(GY)
    index_x = lax.axis_index(GX)
    index_y = lax.axis_index(GY)
    order_here = orders[index_x, index_y]
    own_strips = order_here // STRIP
    live_mask = (jnp.arange(ORDER, dtype=jnp.int32) < order_here).astype(jnp.float32)[None, :]
    multipliers = warm[0, 0] * live_mask
    rhs_here = loads[0, 0] * live_mask
    for iteration in range(ITERS):
        pieces = [
            strip_or_zero(
                strip_number < own_strips,
                multipliers,
                operator_block[strip_number * STRIP : (strip_number + 1) * STRIP],
            )
            for strip_number in range(STRIPS)
        ]
        products = jnp.concatenate(pieces, axis=1)
        near_x = products[:, rows_x]
        sum_x = shift_columns(near_x, 1) + shift_columns(near_x, -1)
        near_y = products[:, rows_y]
        sum_y = shift_rows(near_y, 1) + shift_rows(near_y, -1)
        jumps = products.at[:, rows_x].add(-sum_x).at[:, rows_y].add(-sum_y)
        gradient = jumps - rhs_here
        squares = over_axes(
            jnp.sum(gradient * gradient, axis=1), (("gx_0", "gx_1"), ("gy_0", "gy_1"))
        )
        spread = jnp.sqrt(squares / (count_x * count_y * ORDER) + epsilon)
        multipliers = multipliers - step_length * gradient / spread[:, None]
        multipliers = jnp.where(
            contact_here[None, :] == 1, jnp.maximum(multipliers, 0.0), multipliers
        )
    return multipliers[None, None]


def solution(mesh):
    finer = Mesh(mesh.devices.reshape(16, 2, 4, 4), ("gx_0", "gx_1", "gy_0", "gy_1"))
    in_specs = (
        P(GX, GY, None, None),
        P(GX, GY, None, None),
        P(GX, GY, None, None),
        P(),
        P(GX, GY, None),
        P(GX, GY, None),
        P(GX, GY, None),
    )
    out_specs = P(GX, GY, None, None)
    return jax.shard_map(body, mesh=finer, in_specs=in_specs, out_specs=out_specs, check_vma=False)
```

profile of v0, /device:TPU:1, one launch (start us, length us, event | category | flops | bytes accessed | tf_op | source)
XLA Modules:
  0.0 202.5 jit_solution(9098134895353953753)
XLA Ops:
  6.0 3.0 %slice_bitcast_fusion = (f32[128,768]{1,0:T(8,128)S(1)}, f32[128,768]{1,0:T(8,128)S(1)}, f32[128,768]{1,0:T(8,128)S(1)}, f32[128,768]{1,0:T(8,128)}, f32[128,768]{1,0:T(8,128)}, /*index=5*/f32[128,768]{1,0:T(8,128)S(1)}) fusion(f32[1,1,768,768]{3,2,1,0:T(8,128)} %param.43), kind=kLoop, calls=%fused_computation.24 | loop fusion | bytes 4718592 | tf_op jit(solution)/shard_map/slice | solution.py:87
  9.1 1.8 conditional.18
  15.0 4.3 %collective-permute-start = (f32[256,128]{0,1:T(8,128)}, f32[256,128]{0,1:T(8,128)}, u32[]{:S(2)}, u32[]{:S(2)}) collective-permute-start(f32[256,128]{0,1:T(8,128)} %bitcast.10), channel_id=1, source_target_pairs={{0,16},{16,32},{32,48},{48,64},{64,80},{80,96},{96,112},{112,128},... | collective-permute-start | bytes 393224 | tf_op jit(solution)/shard_map/ppermute | solution.py:22
  19.3 8.0 %collective-permute-start.1 = (f32[256,128]{0,1:T(8,128)}, f32[256,128]{0,1:T(8,128)}, u32[]{:S(2)}, u32[]{:S(2)}) collective-permute-start(f32[256,128]{0,1:T(8,128)} %bitcast.10), channel_id=1, source_target_pairs={{16,0},{32,16},{48,32},{64,48},{80,64},{96,80},{112,96},{128,112},... | collective-permute-start | bytes 393224 | tf_op jit(solution)/shard_map/ppermute | solution.py:22
  28.8 2.1 %collective-permute-start.2 = (f32[256,128]{0,1:T(8,128)}, f32[256,128]{0,1:T(8,128)}, u32[]{:S(2)}, u32[]{:S(2)}) collective-permute-start(f32[256,128]{0,1:T(8,128)} %bitcast.14), channel_id=1, source_target_pairs={{0,1},{1,2},{2,3},{3,4},{4,5},{5,6},{6,7},{7,8},{8,9},{9,10},{10,1... | collective-permute-start | bytes 393224 | tf_op jit(solution)/shard_map/ppermute | solution.py:22
  32.4 2.0 %scatter_custom_fusion = f32[256,768]{0,1:T(8,128)S(1)} fusion(f32[256,768]{0,1:T(8,128)S(1)} %constant_dynamic-update-slice_fusion, s32[128]{0:T(128)} %copy-done.13, f32[256,128]{0,1:T(8,128)} %collective-permute-done, f32[256,128]{0,1:T(8,128)} %collective-permute-done.1), kind=kCustom, calls=%fused_computation.40 | custom fusion | flops 98304 | bytes 1048576 | tf_op jit(solution)/shard_map/scatter-add | solution.py:96
  34.5 3.8 %collective-permute-done.3 = f32[256,128]{0,1:T(8,128)} collective-permute-done((f32[256,128]{0,1:T(8,128)}, f32[256,128]{0,1:T(8,128)}, u32[]{:S(2)}, u32[]{:S(2)}) %collective-permute-start.3) | collective-permute-done | bytes 131104 | tf_op jit(solution)/shard_map/ppermute | solution.py:22
  38.2 2.0 %scatter_custom_fusion.1 = f32[256,768]{0,1:T(8,128)S(1)} fusion(f32[256,768]{0,1:T(8,128)S(1)} %scatter_custom_fusion, s32[128]{0:T(128)S(1)} %fusion.30, f32[256,128]{0,1:T(8,128)} %collective-permute-done.2, f32[256,128]{0,1:T(8,128)} %collective-permute-done.3), kind=kCustom, calls=%fused_computation.38 | custom fusion | flops 98304 | bytes 1048576 | tf_op jit(solution)/shard_map/scatter-add | solution.py:96
  40.5 9.9 %all_to_all.36 = f32[16,1,256]{2,1,0:T(1,128)S(1)} all-to-all(f32[16,1,256]{2,1,0:T(1,128)S(1)} %broadcast_in_dim.52), channel_id=1, replica_groups=mesh['gx_0'=16,'gx_1'=2,'gy_0'=4,'gy_1'=4] {'gy_0','gy_1'}, dimensions={0} | all-to-all | bytes 32768 | tf_op jit(solution)/shard_map/all_to_all | solution.py:27
  51.0 20.2 %all-to-all-start.1 = ((f32[32,1,256]{2,1,0:T(1,128)}), f32[32,1,256]{2,1,0:T(1,128)S(1)}, u32[]{:S(2)}, u32[]{:S(2)}) async-start(f32[32,1,256]{2,1,0:T(1,128)} %broadcast_in_dim.53), calls=%async_computation.1 | async-start | bytes 65536 | tf_op jit(solution)/shard_map/all_to_all | solution.py:27
  71.9 11.4 %all-to-all-done.1 = f32[32,1,256]{2,1,0:T(1,128)S(1)} async-done(((f32[32,1,256]{2,1,0:T(1,128)}), f32[32,1,256]{2,1,0:T(1,128)S(1)}, u32[]{:S(2)}, u32[]{:S(2)}) %all-to-all-start.1) | async-done | bytes 32800 | tf_op jit(solution)/shard_map/all_to_all | solution.py:27
  91.1 1.9 collective-permute-start.4
  93.0 4.1 %collective-permute-start.5 = (f32[256,128]{0,1:T(8,128)S(1)}, f32[256,128]{0,1:T(8,128)S(1)}, u32[]{:S(2)}, u32[]{:S(2)}) collective-permute-start(f32[256,128]{0,1:T(8,128)S(1)} %bitcast.114), channel_id=1, source_target_pairs={{16,0},{32,16},{48,32},{64,48},{80,64},{96,80},{112,96},{128,112},... | collective-permute-start | bytes 393224 | tf_op jit(solution)/shard_map/ppermute | solution.py:22
  97.9 1.8 collective-permute-start.6
  102.8 3.5 %collective-permute-done.7 = f32[256,128]{0,1:T(8,128)S(1)} collective-permute-done((f32[256,128]{0,1:T(8,128)S(1)}, f32[256,128]{0,1:T(8,128)S(1)}, u32[]{:S(2)}, u32[]{:S(2)}) %collective-permute-start.7) | collective-permute-done | bytes 131104 | tf_op jit(solution)/shard_map/ppermute | solution.py:22
  108.3 13.5 %all_to_all.37 = f32[16,1,256]{2,1,0:T(1,128)S(1)} all-to-all(f32[16,1,256]{2,1,0:T(1,128)S(1)} %broadcast_in_dim.54), channel_id=1, replica_groups=mesh['gx_0'=16,'gx_1'=2,'gy_0'=4,'gy_1'=4] {'gy_0','gy_1'}, dimensions={0} | all-to-all | bytes 32768 | tf_op jit(solution)/shard_map/all_to_all | solution.py:27
  122.4 8.0 %all-to-all-start.3 = ((f32[32,1,256]{2,1,0:T(1,128)}), f32[32,1,256]{2,1,0:T(1,128)S(1)}, u32[]{:S(2)}, u32[]{:S(2)}) async-start(f32[32,1,256]{2,1,0:T(1,128)} %broadcast_in_dim.55), calls=%async_computation.3 | async-start | bytes 65536 | tf_op jit(solution)/shard_map/all_to_all | solution.py:27
  130.5 12.1 %all-to-all-done.3 = f32[32,1,256]{2,1,0:T(1,128)S(1)} async-done(((f32[32,1,256]{2,1,0:T(1,128)}), f32[32,1,256]{2,1,0:T(1,128)S(1)}, u32[]{:S(2)}, u32[]{:S(2)}) %all-to-all-start.3) | async-done | bytes 32800 | tf_op jit(solution)/shard_map/all_to_all | solution.py:27
  150.3 1.9 collective-permute-start.8
  152.3 4.2 %collective-permute-start.9 = (f32[256,128]{0,1:T(8,128)S(1)}, f32[256,128]{0,1:T(8,128)S(1)}, u32[]{:S(2)}, u32[]{:S(2)}) collective-permute-start(f32[256,128]{0,1:T(8,128)S(1)} %bitcast.112), channel_id=1, source_target_pairs={{16,0},{32,16},{48,32},{64,48},{80,64},{96,80},{112,96},{128,112},... | collective-permute-start | bytes 393224 | tf_op jit(solution)/shard_map/ppermute | solution.py:22
  157.2 1.9 collective-permute-start.10
  162.1 3.3 %collective-permute-done.11 = f32[256,128]{0,1:T(8,128)S(1)} collective-permute-done((f32[256,128]{0,1:T(8,128)S(1)}, f32[256,128]{0,1:T(8,128)S(1)}, u32[]{:S(2)}, u32[]{:S(2)}) %collective-permute-start.11) | collective-permute-done | bytes 131104 | tf_op jit(solution)/shard_map/ppermute | solution.py:22
  167.4 13.6 %all_to_all.38 = f32[16,1,256]{2,1,0:T(1,128)S(1)} all-to-all(f32[16,1,256]{2,1,0:T(1,128)S(1)} %broadcast_in_dim.56), channel_id=1, replica_groups=mesh['gx_0'=16,'gx_1'=2,'gy_0'=4,'gy_1'=4] {'gy_0','gy_1'}, dimensions={0} | all-to-all | bytes 32768 | tf_op jit(solution)/shard_map/all_to_all | solution.py:27
  181.1 19.9 %all_to_all.39 = f32[32,1,256]{2,1,0:T(1,128)S(1)} all-to-all(f32[32,1,256]{2,1,0:T(1,128)S(1)} %broadcast_in_dim.57), channel_id=1, replica_groups=mesh['gx_0'=16,'gx_1'=2,'gy_0'=4,'gy_1'=4] {'gx_0','gx_1'}, dimensions={0} | all-to-all | bytes 65536 | tf_op jit(solution)/shard_map/all_to_all | solution.py:27
  (138 shorter events, 54.4 us)
Async XLA Ops:
  8.9 3.8 %copy-start.8 = (f32[128,768]{1,0:T(8,128)}, f32[128,768]{1,0:T(8,128)S(1)}, u32[]{:S(2)}) copy-start(f32[128,768]{1,0:T(8,128)S(1)} %get-tuple-element.295) | copy-start | bytes 1179652
  8.9 4.4 %copy-start.5 = (f32[128,768]{1,0:T(8,128)}, f32[128,768]{1,0:T(8,128)S(1)}, u32[]{:S(2)}) copy-start(f32[128,768]{1,0:T(8,128)S(1)} %get-tuple-element.294) | copy-start | bytes 1179652
  8.9 4.5 %copy-start.2 = (f32[128,768]{1,0:T(8,128)}, f32[128,768]{1,0:T(8,128)S(1)}, u32[]{:S(2)}) copy-start(f32[128,768]{1,0:T(8,128)S(1)} %get-tuple-element.298) | copy-start | bytes 1179652
  11.1 27.2 %copy-start.12 = (s32[128]{0:T(128)}, s32[128]{0:T(128)S(1)}, u32[]{:S(2)}) copy-start(s32[128]{0:T(128)S(1)} %fusion.30) | copy-start | bytes 1540
  13.5 18.7 %copy-start.9 = (f32[1,1,256,768]{3,2,1,0:T(8,128)S(1)}, f32[1,1,256,768]{3,2,1,0:T(8,128)}, u32[]{:S(2)}) copy-start(f32[1,1,256,768]{3,2,1,0:T(8,128)} %param.44) | copy-start | bytes 2359300
  15.0 17.4 %collective-permute-start = (f32[256,128]{0,1:T(8,128)}, f32[256,128]{0,1:T(8,128)}, u32[]{:S(2)}, u32[]{:S(2)}) collective-permute-start(f32[256,128]{0,1:T(8,128)} %bitcast.10), channel_id=1, source_target_pairs={{0,16},{16,32},{32,48},{48,64},{64,80},{80,96},{96,112},{112,128},... | collective-permute-start | bytes 393224 | tf_op jit(solution)/shard_map/ppermute | solution.py:22
  19.3 13.1 %collective-permute-start.1 = (f32[256,128]{0,1:T(8,128)}, f32[256,128]{0,1:T(8,128)}, u32[]{:S(2)}, u32[]{:S(2)}) collective-permute-start(f32[256,128]{0,1:T(8,128)} %bitcast.10), channel_id=1, source_target_pairs={{16,0},{32,16},{48,32},{64,48},{80,64},{96,80},{112,96},{128,112},... | collective-permute-start | bytes 393224 | tf_op jit(solution)/shard_map/ppermute | solution.py:22
  28.8 54.6 %copy-start.1 = (f32[1,1,256,768]{2,3,1,0:T(8,128)S(1)}, f32[1,1,256,768]{2,3,1,0:T(8,128)}, u32[]{:S(2)}) copy-start(f32[1,1,256,768]{2,3,1,0:T(8,128)} %copy-done) | copy-start | bytes 2359300
  28.8 5.7 %collective-permute-start.2 = (f32[256,128]{0,1:T(8,128)}, f32[256,128]{0,1:T(8,128)}, u32[]{:S(2)}, u32[]{:S(2)}) collective-permute-start(f32[256,128]{0,1:T(8,128)} %bitcast.14), channel_id=1, source_target_pairs={{0,1},{1,2},{2,3},{3,4},{4,5},{5,6},{6,7},{7,8},{8,9},{9,10},{10,1... | collective-permute-start | bytes 393224 | tf_op jit(solution)/shard_map/ppermute | solution.py:22
  30.8 7.4 %collective-permute-start.3 = (f32[256,128]{0,1:T(8,128)}, f32[256,128]{0,1:T(8,128)}, u32[]{:S(2)}, u32[]{:S(2)}) collective-permute-start(f32[256,128]{0,1:T(8,128)} %bitcast.14), channel_id=1, source_target_pairs={{1,0},{2,1},{3,2},{4,3},{5,4},{6,5},{7,6},{8,7},{9,8},{10,9},{11,1... | collective-permute-start | bytes 393224 | tf_op jit(solution)/shard_map/ppermute | solution.py:22
  51.0 32.3 %all-to-all-start.1 = ((f32[32,1,256]{2,1,0:T(1,128)}), f32[32,1,256]{2,1,0:T(1,128)S(1)}, u32[]{:S(2)}, u32[]{:S(2)}) async-start(f32[32,1,256]{2,1,0:T(1,128)} %broadcast_in_dim.53), calls=%async_computation.1 | async-start | bytes 65536 | tf_op jit(solution)/shard_map/all_to_all | solution.py:27
  83.6 5.6 %copy-start.6 = (f32[128,768]{1,0:T(8,128)S(1)}, f32[128,768]{1,0:T(8,128)}, u32[]{:S(2)}) copy-start(f32[128,768]{1,0:T(8,128)} %copy-done.5) | copy-start | bytes 1179652
  85.3 4.9 %copy-start.3 = (f32[128,768]{1,0:T(8,128)S(1)}, f32[128,768]{1,0:T(8,128)}, u32[]{:S(2)}) copy-start(f32[128,768]{1,0:T(8,128)} %copy-done.2) | copy-start | bytes 1179652
  91.1 10.0 %collective-permute-start.4 = (f32[256,128]{0,1:T(8,128)S(1)}, f32[256,128]{0,1:T(8,128)S(1)}, u32[]{:S(2)}, u32[]{:S(2)}) collective-permute-start(f32[256,128]{0,1:T(8,128)S(1)} %bitcast.113), channel_id=1, source_target_pairs={{0,16},{16,32},{32,48},{48,64},{64,80},{80,96},{96,112},{112,128},... | collective-permute-start | bytes 393224 | tf_op jit(solution)/shard_map/ppermute | solution.py:22
  93.0 8.1 %collective-permute-start.5 = (f32[256,128]{0,1:T(8,128)S(1)}, f32[256,128]{0,1:T(8,128)S(1)}, u32[]{:S(2)}, u32[]{:S(2)}) collective-permute-start(f32[256,128]{0,1:T(8,128)S(1)} %bitcast.114), channel_id=1, source_target_pairs={{16,0},{32,16},{48,32},{64,48},{80,64},{96,80},{112,96},{128,112},... | collective-permute-start | bytes 393224 | tf_op jit(solution)/shard_map/ppermute | solution.py:22
  97.9 4.9 %collective-permute-start.6 = (f32[256,128]{0,1:T(8,128)S(1)}, f32[256,128]{0,1:T(8,128)S(1)}, u32[]{:S(2)}, u32[]{:S(2)}) collective-permute-start(f32[256,128]{0,1:T(8,128)S(1)} %bitcast.109), channel_id=1, source_target_pairs={{0,1},{1,2},{2,3},{3,4},{4,5},{5,6},{6,7},{7,8},{8,9},{9,10},{10,1... | collective-permute-start | bytes 393224 | tf_op jit(solution)/shard_map/ppermute | solution.py:22
  99.8 6.6 %collective-permute-start.7 = (f32[256,128]{0,1:T(8,128)S(1)}, f32[256,128]{0,1:T(8,128)S(1)}, u32[]{:S(2)}, u32[]{:S(2)}) collective-permute-start(f32[256,128]{0,1:T(8,128)S(1)} %bitcast.110), channel_id=1, source_target_pairs={{1,0},{2,1},{3,2},{4,3},{5,4},{6,5},{7,6},{8,7},{9,8},{10,9},{11,1... | collective-permute-start | bytes 393224 | tf_op jit(solution)/shard_map/ppermute | solution.py:22
  122.4 20.1 %all-to-all-start.3 = ((f32[32,1,256]{2,1,0:T(1,128)}), f32[32,1,256]{2,1,0:T(1,128)S(1)}, u32[]{:S(2)}, u32[]{:S(2)}) async-start(f32[32,1,256]{2,1,0:T(1,128)} %broadcast_in_dim.55), calls=%async_computation.3 | async-start | bytes 65536 | tf_op jit(solution)/shard_map/all_to_all | solution.py:27
  142.9 5.6 %copy-start.7 = (f32[128,768]{1,0:T(8,128)S(1)}, f32[128,768]{1,0:T(8,128)}, u32[]{:S(2)}) copy-start(f32[128,768]{1,0:T(8,128)} %copy-done.5) | copy-start | bytes 1179652
  144.5 4.9 %copy-start.4 = (f32[128,768]{1,0:T(8,128)S(1)}, f32[128,768]{1,0:T(8,128)}, u32[]{:S(2)}) copy-start(f32[128,768]{1,0:T(8,128)} %copy-done.2) | copy-start | bytes 1179652
  150.3 10.0 %collective-permute-start.8 = (f32[256,128]{0,1:T(8,128)S(1)}, f32[256,128]{0,1:T(8,128)S(1)}, u32[]{:S(2)}, u32[]{:S(2)}) collective-permute-start(f32[256,128]{0,1:T(8,128)S(1)} %bitcast.111), channel_id=1, source_target_pairs={{0,16},{16,32},{32,48},{48,64},{64,80},{80,96},{96,112},{112,128},... | collective-permute-start | bytes 393224 | tf_op jit(solution)/shard_map/ppermute | solution.py:22
  152.3 8.1 %collective-permute-start.9 = (f32[256,128]{0,1:T(8,128)S(1)}, f32[256,128]{0,1:T(8,128)S(1)}, u32[]{:S(2)}, u32[]{:S(2)}) collective-permute-start(f32[256,128]{0,1:T(8,128)S(1)} %bitcast.112), channel_id=1, source_target_pairs={{16,0},{32,16},{48,32},{64,48},{80,64},{96,80},{112,96},{128,112},... | collective-permute-start | bytes 393224 | tf_op jit(solution)/shard_map/ppermute | solution.py:22
  157.2 4.9 %collective-permute-start.10 = (f32[256,128]{0,1:T(8,128)S(1)}, f32[256,128]{0,1:T(8,128)S(1)}, u32[]{:S(2)}, u32[]{:S(2)}) collective-permute-start(f32[256,128]{0,1:T(8,128)S(1)} %bitcast.107), channel_id=1, source_target_pairs={{0,1},{1,2},{2,3},{3,4},{4,5},{5,6},{6,7},{7,8},{8,9},{9,10},{10,1... | collective-permute-start | bytes 393224 | tf_op jit(solution)/shard_map/ppermute | solution.py:22
  159.0 6.4 %collective-permute-start.11 = (f32[256,128]{0,1:T(8,128)S(1)}, f32[256,128]{0,1:T(8,128)S(1)}, u32[]{:S(2)}, u32[]{:S(2)}) collective-permute-start(f32[256,128]{0,1:T(8,128)S(1)} %bitcast.108), channel_id=1, source_target_pairs={{1,0},{2,1},{3,2},{4,3},{5,4},{6,5},{7,6},{8,7},{9,8},{10,9},{11,1... | collective-permute-start | bytes 393224 | tf_op jit(solution)/shard_map/ppermute | solution.py:22
  (6 other events, 10.9 us)
where the time goes:
time: 203 us; the launch traced here: 202 us
  starting transfers between devices  62.4 us (31%)
  blocking collectives  56.8 us (28%)
  waiting for transfers between devices  34.1 us (17%)
  local copies, waits for them, and re-layouts  17.7 us (9%)
  other arithmetic  14.2 us (7%)
  matrix products  13.5 us (7%)
  between operations  3.46 us (2%)
    all_to_all x4, blocking collectives, from_everyone(): return lax.all_to_all(copies, axis, split_axis=0, concat_axis=0, tiled=True)  56.8 us
    ppermute x12, starting transfers between devices, passed_along(): return lax.ppermute(block, axis, route)  34.1 us
    all_to_all x2, starting transfers between devices, from_everyone(): return lax.all_to_all(copies, axis, split_axis=0, concat_axis=0, tiled=True)  28.2 us
    all_to_all x2, waiting for transfers between devices, from_everyone(): return lax.all_to_all(copies, axis, split_axis=0, concat_axis=0, tiled=True)  23.4 us
    cond x9, matrix products, strip_or_zero(): lax.cond(active, lambda operands: strip_product(operands[0], operands[1])...  13.5 us
    scatter-add x6, other arithmetic, body(): jumps = products.at[:, rows_x].add(-sum_x).at[:, rows_y].add(-sum_y)  10.9 us
    ppermute x12, waiting for transfers between devices, passed_along(): return lax.ppermute(block, axis, route)  10.6 us
    unnamed x49, local copies, waits for them, and re-layouts  5.01 us
  transfers between devices with their start and end apart: 14, of which 5 were waited for; matrix products, arithmetic and copies ran while one was open for 5% of the time, Pallas kernels for 0%

commit v1 on v0

v1 whole, which is shorter than its diff:
```python
import jax
import jax.numpy as jnp
from jax import lax
from jax.experimental import pallas as pl
from jax.experimental.pallas import tpu as pltpu
from jax.sharding import Mesh
from jax.sharding import PartitionSpec as P

ORDER = 768
FSLOT = 128
COLS = 256
ITERS = 3
GX = ("z", "c")
GY = ("y", "x")
NEAR = ("c", "y", "x")
FAR = ("z",)

step_length = 0.5
epsilon = 1e-06

f32 = jnp.float32
bf16 = jnp.bfloat16


def dot(a, b):
    return lax.dot_general(a, b, (((1,), (0,)), ((), ())), preferred_element_type=f32)


def split(x):
    high = x.astype(bf16)
    return high, (x - high.astype(f32)).astype(bf16)


def product(a_high, a_low, m_high, m_low):
    return dot(a_high, m_high) + (dot(a_high, m_low) + dot(a_low, m_high))


def live_rows(order, columns):
    return lax.broadcasted_iota(jnp.int32, (ORDER, columns), 0) < order


def first_kernel(place, orders, operator, warm, face_x, face_y,
                 high_out, low_out, faces_high_out, faces_low_out, spots_out, m_out, m_high_out, m_low_out, near_x_out, near_y_out):
    order = orders[place[1], place[0]]
    m = jnp.where(live_rows(order, COLS), warm[...].T, 0.0)
    m_out[...] = m
    m_high, m_low = split(m)
    m_high_out[...] = m_high
    m_low_out[...] = m_low
    high, low = split(jnp.where(live_rows(order, ORDER), operator[...], 0.0))
    high_out[...] = high
    low_out[...] = low
    rows = lax.broadcasted_iota(jnp.int32, (ORDER, FSLOT), 0)
    spots_out[:, :FSLOT] = jnp.where(rows == face_x[...], 1.0, 0.0).astype(bf16)
    spots_out[:, FSLOT:] = jnp.where(rows == face_y[...], 1.0, 0.0).astype(bf16)
    for number, (face, near_out) in enumerate(((face_x, near_x_out), (face_y, near_y_out))):
        column = jnp.broadcast_to(face[...].astype(f32), (FSLOT, FSLOT)).T
        wide = jnp.concatenate([column] * (ORDER // FSLOT), axis=1)
        lanes = lax.broadcasted_iota(jnp.int32, (FSLOT, ORDER), 1).astype(f32)
        pick = jnp.where(wide == lanes, 1.0, 0.0).astype(bf16)
        face_high = dot(pick, high).astype(bf16)
        face_low = dot(pick, low).astype(bf16)
        faces_high_out[number * FSLOT : (number + 1) * FSLOT, :] = face_high
        faces_low_out[number * FSLOT : (number + 1) * FSLOT, :] = face_low
        near_out[...] = product(face_high, face_low, m_high, m_low)


def first_main_kernel(place, orders, high, low, m_high, m_low, loads, contact, local_out, rhs_out, floor_out):
    order = orders[place[1], place[0]]
    rhs = jnp.where(live_rows(order, COLS), loads[...].T, 0.0)
    rhs_out[...] = rhs
    floor = jnp.where(contact[...] == 1, 0.0, -jnp.inf)
    floor_out[...] = jnp.broadcast_to(floor, (FSLOT, ORDER)).T
    local_out[...] = product(high[...], low[...], m_high[...], m_low[...]) - rhs


def main_kernel(high, low, m_high, m_low, rhs, local_out):
    local_out[...] = product(high[...], low[...], m_high[...], m_low[...]) - rhs[...]


def gradient_kernel(local, spots, left, right, below, above, gradient_out, squares_out):
    sums = jnp.concatenate([left[...] + right[...], below[...] + above[...]], axis=0)
    sum_high, sum_low = split(sums)
    gradient = local[...] - (dot(spots[...], sum_high) + dot(spots[...], sum_low))
    gradient_out[...] = gradient
    squares_out[...] = jnp.sum(gradient * gradient, axis=0, keepdims=True)


def updated(everything, m, gradient, floor, count):
    squares = jnp.sum(everything[...], axis=0)
    rate = step_length / jnp.sqrt(squares / count + epsilon)
    lowest = jnp.concatenate([floor[...]] * (COLS // FSLOT), axis=1)
    return jnp.maximum(m[...] - gradient[...] * rate, lowest)


def update_kernel(count, everything, m, gradient, floor, faces_high, faces_low, m_out, m_high_out, m_low_out, near_x_out, near_y_out):
    new = updated(everything, m, gradient, floor, count)
    m_out[...] = new
    m_high, m_low = split(new)
    m_high_out[...] = m_high
    m_low_out[...] = m_low
    near = product(faces_high[...], faces_low[...], m_high, m_low)
    near_x_out[...] = near[:FSLOT]
    near_y_out[...] = near[FSLOT:]


def last_kernel(count, everything, m, gradient, floor, out):
    out[...] = updated(everything, m, gradient, floor, count).T


VMEM = pl.BlockSpec(memory_space=pltpu.VMEM)
SMEM = pl.BlockSpec(memory_space=pltpu.SMEM)


def call(kernel, name, out, *args, scalars=0):
    shapes = tuple(pltpu.VMEM(shape, dtype) for shape, dtype in out)
    args = [*args[:scalars], *(pltpu.with_memory_space_constraint(arg, pltpu.VMEM) for arg in args[scalars:])]
    result = pl.pallas_call(
        kernel,
        name=name,
        out_shape=shapes,
        in_specs=[SMEM] * scalars + [VMEM] * (len(args) - scalars),
        out_specs=tuple(VMEM for _ in shapes),
        compiler_params=pltpu.CompilerParams(vmem_limit_bytes=24 * 2**20),
    )(*args)
    return result


def passed_along(block, axis, distance):
    devices = range(lax.axis_size(axis))
    route = [(i - distance, i) for i in devices if i - distance in devices]
    return lax.ppermute(block, axis, route)


def from_everyone(x, axis):
    copies = jnp.broadcast_to(x[None], (lax.axis_size(axis), *x.shape))
    return lax.all_to_all(copies, axis, split_axis=0, concat_axis=0, tiled=True)


def body(operator, loads, warm, orders, face_x, face_y, contact):
    count = float(lax.axis_size(GX) * lax.axis_size(GY) * ORDER)
    place = jnp.stack([lax.axis_index(GX), lax.axis_index(GY)]).astype(jnp.int32)
    square = ((ORDER, ORDER), bf16)
    faces = ((2 * FSLOT, ORDER), bf16)
    state = ((ORDER, COLS), f32)
    half = ((ORDER, COLS), bf16)
    face = ((FSLOT, COLS), f32)
    high, low, faces_high, faces_low, spots, m, m_high, m_low, near_x, near_y = call(
        first_kernel, "first",
        [square, square, faces, faces, ((ORDER, 2 * FSLOT), bf16), state, half, half, face, face],
        place, orders.T, operator[0, 0], warm[0, 0], face_x[0], face_y[0], scalars=2,
    )
    for iteration in range(ITERS):
        below = passed_along(near_y, GY, 1)
        above = passed_along(near_y, GY, -1)
        left = passed_along(near_x, GX, 1)
        right = passed_along(near_x, GX, -1)
        if iteration == 0:
            local, rhs, floor = call(
                first_main_kernel, "first_main", [state, state, ((ORDER, FSLOT), f32)],
                place, orders.T, high, low, m_high, m_low, loads[0, 0], contact[0], scalars=2,
            )
        else:
            (local,) = call(main_kernel, "main", [state], high, low, m_high, m_low, rhs)
        gradient, squares = call(
            gradient_kernel, "gradient", [state, ((1, COLS), f32)], local, spots, left, right, below, above
        )
        squares = jnp.sum(from_everyone(squares, NEAR), axis=0)
        everything = from_everyone(squares, FAR)
        if iteration < ITERS - 1:
            m, m_high, m_low, near_x, near_y = call(
                lambda *refs: update_kernel(count, *refs), "update", [state, half, half, face, face],
                everything, m, gradient, floor, faces_high, faces_low,
            )
        else:
            (out,) = call(lambda *refs: last_kernel(count, *refs), "last", [((COLS, ORDER), f32)], everything, m, gradient, floor)
    return out[None, None]


def solution(mesh):
    shape = dict(mesh.shape)
    finer = Mesh(mesh.devices.reshape(shape["gx"] // 2, 2, 4, shape["gy"] // 4), ("z", "c", "y", "x"))
    in_specs = (
        P(GX, GY, None, None),
        P(GX, GY, None, None),
        P(GX, GY, None, None),
        P(),
        P(GX, GY, None),
        P(GX, GY, None),
        P(GX, GY, None),
    )
    out_specs = P(GX, GY, None, None)
    return jax.shard_map(body, mesh=finer, in_specs=in_specs, out_specs=out_specs, check_vma=False)
```

time: 203 us -> 169 us (0.83)
  blocking collectives: 56.8 us -> 98.4 us
  waiting for transfers between devices: 34.1 us -> 2.4 us
  starting transfers between devices: 62.4 us -> 38.8 us
  matrix products: 13.5 us -> 0 us
  other arithmetic: 14.2 us -> 1.75 us
  Pallas kernels: 0 us -> 9.18 us
  between operations: 3.46 us -> 0.35 us
    all_to_all x4 -> x6, blocking collectives: 56.8 us -> 98.4 us  [from_everyone(): return lax.all_to_all(copies, axis, split_axis=0, concat_axis=0, tiled=True)]
    all_to_all x2 -> x0, starting transfers between devices: 28.2 us -> none  [from_everyone(): return lax.all_to_all(copies, axis, split_axis=0, concat_axis=0, tiled=True)]
    all_to_all x2 -> x0, waiting for transfers between devices: 23.4 us -> none  [from_everyone(): return lax.all_to_all(copies, axis, split_axis=0, concat_axis=0, tiled=True)]
    cond x9 -> x0, matrix products: 13.5 us -> none  [strip_or_zero(): lax.cond(active, lambda operands: strip_product(operands[0], operands[1])...]
    unnamed x49 -> x47, local copies, waits for them, and re-layouts: 5.01 us -> 16.6 us
    scatter-add x6 -> x0, other arithmetic: 10.9 us -> none  [body(): jumps = products.at[:, rows_x].add(-sum_x).at[:, rows_y].add(-sum_y)]
    pallas_call x0 -> x10, Pallas kernels: none -> 9.18 us  [call(): pl.pallas_call(kernel, name=name, out_shape=shapes, in_specs=[SMEM] * sca...]
    ppermute x12, waiting for transfers between devices: 10.6 us -> 2.4 us  [passed_along(): return lax.ppermute(block, axis, route)]
  transfers between devices with their start and end apart: 14 -> 12, of which waited for: 5 -> 4; matrix products, arithmetic and copies ran while one was open for 5% -> 0% of each run, Pallas kernels for 0% -> 2%
where the time goes in v1:
time: 169 us; the launch traced here: 168 us
  blocking collectives  98.4 us (58%)
  starting transfers between devices  38.8 us (23%)
  local copies, waits for them, and re-layouts  16.7 us (10%)
  Pallas kernels  9.18 us (5%)
  waiting for transfers between devices  2.4 us (1%)
  other arithmetic  1.75 us (1%)
    all_to_all x6, blocking collectives, from_everyone(): return lax.all_to_all(copies, axis, split_axis=0, concat_axis=0, tiled=True)  98.4 us
    ppermute x12, starting transfers between devices, passed_along(): return lax.ppermute(block, axis, route)  38.8 us
    unnamed x47, local copies, waits for them, and re-layouts  16.6 us
    pallas_call x10, Pallas kernels, call(): pl.pallas_call(kernel, name=name, out_shape=shapes, in_specs=[SMEM] * sca...  9.18 us
  transfers between devices with their start and end apart: 12, of which 4 were waited for; matrix products, arithmetic and copies ran while one was open for 0% of the time, Pallas kernels for 2%

profile of v1, /device:TPU:1, one launch (start us, length us, event | category | flops | bytes accessed | tf_op | source)
XLA Modules:
  0.0 167.6 jit_solution(12614456819799886733)
XLA Ops:
  0.1 1.7 copy-done.3
  1.7 1.1 copy-done.7
  4.9 2.6 %first.1 = (bf16[768,768]{1,0:T(8,128)(2,1)S(1)}, bf16[768,768]{1,0:T(8,128)(2,1)S(1)}, bf16[256,768]{1,0:T(8,128)(2,1)S(1)}, bf16[256,768]{1,0:T(8,128)(2,1)S(1...) custom-call(s32[2]{0:T(128)S(1)} %pad_add_fusion.place, ...), custom_call_target="tpu_custom_call" | custom-call | tf_op jit(solution)/shard_map/first/pallas_call | solution.py:118
  9.1 8.7 %collective-permute-start.1 = (f32[128,256]{1,0:T(8,128)S(1)}, f32[128,256]{1,0:T(8,128)S(1)}, u32[]{:S(2)}, u32[]{:S(2)}) collective-permute-start(f32[128,256]{1,0:T(8,128)S(1)} %get-tuple-element.40), channel_id=1, source_target_pairs={{16,0},{32,16},{48,32},{64,48},{80,64},{96,80},{112,96},{128,112},... | collective-permute-start | bytes 393224 | tf_op jit(solution)/shard_map/ppermute | solution.py:132
  17.8 1.9 %collective-permute-start = (f32[128,256]{1,0:T(8,128)S(1)}, f32[128,256]{1,0:T(8,128)S(1)}, u32[]{:S(2)}, u32[]{:S(2)}) collective-permute-start(f32[128,256]{1,0:T(8,128)S(1)} %get-tuple-element.40), channel_id=1, source_target_pairs={{0,16},{16,32},{32,48},{48,64},{64,80},{80,96},{96,112},{112,128},... | collective-permute-start | bytes 393224 | tf_op jit(solution)/shard_map/ppermute | solution.py:132
  19.8 1.3 collective-permute-start.3
  21.1 4.0 %collective-permute-start.2 = (f32[128,256]{1,0:T(8,128)S(1)}, f32[128,256]{1,0:T(8,128)S(1)}, u32[]{:S(2)}, u32[]{:S(2)}) collective-permute-start(f32[128,256]{1,0:T(8,128)S(1)} %get-tuple-element.41), channel_id=1, source_target_pairs={{0,1},{1,2},{2,3},{3,4},{4,5},{5,6},{6,7},{7,8},{8,9},{9,10},{10,1... | collective-permute-start | bytes 393224 | tf_op jit(solution)/shard_map/ppermute | solution.py:132
  25.1 1.8 %first_main.1 = (f32[768,256]{1,0:T(8,128)S(1)}, f32[768,256]{1,0:T(8,128)S(1)}, f32[768,128]{1,0:T(8,128)S(1)}) custom-call(s32[2]{0:T(128)S(1)} %pad_add_fusion.place, s32[16,32]{1,0:T(8,128)S(1)} %bitcast.18, bf16[768,768]{1,0:T(8,128)(2,1)S(1)} %get-tuple-element.34.high, bf16[768,768]{1,0:T(8,128)(2,1)S(1)} %get-tuple-element.35.low, ...), custom_call_target="tpu_custom_call" | custom-call | tf_op jit(solution)/shard_map/first_main/pallas_call | solution.py:118
  29.1 13.4 %all_to_all.30 = f32[32,1,256]{2,1,0:T(1,128)} all-to-all(f32[32,1,256]{2,1,0:T(1,128)S(1)} %broadcast_in_dim.21), channel_id=1, replica_groups=mesh['z'=16,'c'=2,'y'=4,'x'=4] {'c','y','x'}, dimensions={0} | all-to-all | bytes 65536 | tf_op jit(solution)/shard_map/all_to_all | solution.py:137
  43.4 26.2 %all_to_all.31.refs_0_ = f32[16,1,256]{2,1,0:T(1,128)S(1)} all-to-all(f32[16,1,256]{2,1,0:T(1,128)S(1)} %broadcast_in_dim.22), channel_id=1, replica_groups=mesh['z'=16,'c'=2,'y'=4,'x'=4] {'z'}, dimensions={0} | all-to-all | bytes 32768 | tf_op jit(solution)/shard_map/all_to_all | solution.py:137
  70.6 1.1 copy-done.10
  73.5 4.0 %collective-permute-start.5 = (f32[128,256]{1,0:T(8,128)S(1)}, f32[128,256]{1,0:T(8,128)S(1)}, u32[]{:S(2)}, u32[]{:S(2)}) collective-permute-start(f32[128,256]{1,0:T(8,128)S(1)} %get-tuple-element.51), channel_id=1, source_target_pairs={{16,0},{32,16},{48,32},{64,48},{80,64},{96,80},{112,96},{128,112},... | collective-permute-start | bytes 393224 | tf_op jit(solution)/shard_map/ppermute | solution.py:132
  77.5 2.2 %collective-permute-start.4 = (f32[128,256]{1,0:T(8,128)S(1)}, f32[128,256]{1,0:T(8,128)S(1)}, u32[]{:S(2)}, u32[]{:S(2)}) collective-permute-start(f32[128,256]{1,0:T(8,128)S(1)} %get-tuple-element.51), channel_id=1, source_target_pairs={{0,16},{16,32},{32,48},{48,64},{64,80},{80,96},{96,112},{112,128},... | collective-permute-start | bytes 393224 | tf_op jit(solution)/shard_map/ppermute | solution.py:132
  79.7 1.3 collective-permute-start.7
  81.0 4.0 %collective-permute-start.6 = (f32[128,256]{1,0:T(8,128)S(1)}, f32[128,256]{1,0:T(8,128)S(1)}, u32[]{:S(2)}, u32[]{:S(2)}) collective-permute-start(f32[128,256]{1,0:T(8,128)S(1)} %get-tuple-element.52), channel_id=1, source_target_pairs={{0,1},{1,2},{2,3},{3,4},{4,5},{5,6},{6,7},{7,8},{8,9},{9,10},{10,1... | collective-permute-start | bytes 393224 | tf_op jit(solution)/shard_map/ppermute | solution.py:132
  88.7 15.6 %all_to_all.32 = f32[32,1,256]{2,1,0:T(1,128)} all-to-all(f32[32,1,256]{2,1,0:T(1,128)S(1)} %broadcast_in_dim.24), channel_id=1, replica_groups=mesh['z'=16,'c'=2,'y'=4,'x'=4] {'c','y','x'}, dimensions={0} | all-to-all | bytes 65536 | tf_op jit(solution)/shard_map/all_to_all | solution.py:137
  105.1 13.8 %all_to_all.33.refs_0_ = f32[16,1,256]{2,1,0:T(1,128)S(1)} all-to-all(f32[16,1,256]{2,1,0:T(1,128)S(1)} %broadcast_in_dim.50), channel_id=1, replica_groups=mesh['z'=16,'c'=2,'y'=4,'x'=4] {'z'}, dimensions={0} | all-to-all | bytes 32768 | tf_op jit(solution)/shard_map/all_to_all | solution.py:137
  119.9 1.1 copy-done.12
  122.8 4.0 %collective-permute-start.9 = (f32[128,256]{1,0:T(8,128)S(1)}, f32[128,256]{1,0:T(8,128)S(1)}, u32[]{:S(2)}, u32[]{:S(2)}) collective-permute-start(f32[128,256]{1,0:T(8,128)S(1)} %get-tuple-element.58), channel_id=1, source_target_pairs={{16,0},{32,16},{48,32},{64,48},{80,64},{96,80},{112,96},{128,112},... | collective-permute-start | bytes 393224 | tf_op jit(solution)/shard_map/ppermute | solution.py:132
  126.8 2.2 %collective-permute-start.8 = (f32[128,256]{1,0:T(8,128)S(1)}, f32[128,256]{1,0:T(8,128)S(1)}, u32[]{:S(2)}, u32[]{:S(2)}) collective-permute-start(f32[128,256]{1,0:T(8,128)S(1)} %get-tuple-element.58), channel_id=1, source_target_pairs={{0,16},{16,32},{32,48},{48,64},{64,80},{80,96},{96,112},{112,128},... | collective-permute-start | bytes 393224 | tf_op jit(solution)/shard_map/ppermute | solution.py:132
  129.0 1.3 collective-permute-start.11
  130.3 4.0 %collective-permute-start.10 = (f32[128,256]{1,0:T(8,128)S(1)}, f32[128,256]{1,0:T(8,128)S(1)}, u32[]{:S(2)}, u32[]{:S(2)}) collective-permute-start(f32[128,256]{1,0:T(8,128)S(1)} %get-tuple-element.59), channel_id=1, source_target_pairs={{0,1},{1,2},{2,3},{3,4},{4,5},{5,6},{6,7},{7,8},{8,9},{9,10},{10,1... | collective-permute-start | bytes 393224 | tf_op jit(solution)/shard_map/ppermute | solution.py:132
  137.0 15.5 %all_to_all.34 = f32[32,1,256]{2,1,0:T(1,128)S(1)} all-to-all(f32[32,1,256]{2,1,0:T(1,128)S(1)} %broadcast_in_dim.52), channel_id=1, replica_groups=mesh['z'=16,'c'=2,'y'=4,'x'=4] {'c','y','x'}, dimensions={0} | all-to-all | bytes 65536 | tf_op jit(solution)/shard_map/all_to_all | solution.py:137
  152.6 13.8 %all_to_all.35.refs_0_ = f32[16,1,256]{2,1,0:T(1,128)S(1)} all-to-all(f32[16,1,256]{2,1,0:T(1,128)S(1)} %broadcast_in_dim.53), channel_id=1, replica_groups=mesh['z'=16,'c'=2,'y'=4,'x'=4] {'z'}, dimensions={0} | all-to-all | bytes 32768 | tf_op jit(solution)/shard_map/all_to_all | solution.py:137
  (73 shorter events, 20.6 us)
Async XLA Ops:
  0.1 1.7 copy-start.3
  1.7 1.1 copy-start.7
  4.9 20.2 %copy-start.8 = (f32[1,1,256,768]{3,2,1,0:T(8,128)S(1)}, f32[1,1,256,768]{3,2,1,0:T(8,128)}, u32[]{:S(2)}) copy-start(f32[1,1,256,768]{3,2,1,0:T(8,128)} %param.8) | copy-start | bytes 2359300
  4.9 20.2 %copy-start.20 = (s32[1,1,768]{2,1,0:T(1,128)S(1)}, s32[1,1,768]{2,1,0:T(1,128)}, u32[]{:S(2)}) copy-start(s32[1,1,768]{2,1,0:T(1,128)} %param.13) | copy-start | bytes 9220
  9.1 18.7 %collective-permute-start.1 = (f32[128,256]{1,0:T(8,128)S(1)}, f32[128,256]{1,0:T(8,128)S(1)}, u32[]{:S(2)}, u32[]{:S(2)}) collective-permute-start(f32[128,256]{1,0:T(8,128)S(1)} %get-tuple-element.40), channel_id=1, source_target_pairs={{16,0},{32,16},{48,32},{64,48},{80,64},{96,80},{112,96},{128,112},... | collective-permute-start | bytes 393224 | tf_op jit(solution)/shard_map/ppermute | solution.py:132
  17.8 9.9 %collective-permute-start = (f32[128,256]{1,0:T(8,128)S(1)}, f32[128,256]{1,0:T(8,128)S(1)}, u32[]{:S(2)}, u32[]{:S(2)}) collective-permute-start(f32[128,256]{1,0:T(8,128)S(1)} %get-tuple-element.40), channel_id=1, source_target_pairs={{0,16},{16,32},{32,48},{48,64},{64,80},{80,96},{96,112},{112,128},... | collective-permute-start | bytes 393224 | tf_op jit(solution)/shard_map/ppermute | solution.py:132
  19.8 8.0 %collective-permute-start.3 = (f32[128,256]{1,0:T(8,128)S(1)}, f32[128,256]{1,0:T(8,128)S(1)}, u32[]{:S(2)}, u32[]{:S(2)}) collective-permute-start(f32[128,256]{1,0:T(8,128)S(1)} %get-tuple-element.41), channel_id=1, source_target_pairs={{1,0},{2,1},{3,2},{4,3},{5,4},{6,5},{7,6},{8,7},{9,8},{10,9},{11,1... | collective-permute-start | bytes 393224 | tf_op jit(solution)/shard_map/ppermute | solution.py:132
  21.1 6.7 %collective-permute-start.2 = (f32[128,256]{1,0:T(8,128)S(1)}, f32[128,256]{1,0:T(8,128)S(1)}, u32[]{:S(2)}, u32[]{:S(2)}) collective-permute-start(f32[128,256]{1,0:T(8,128)S(1)} %get-tuple-element.41), channel_id=1, source_target_pairs={{0,1},{1,2},{2,3},{3,4},{4,5},{5,6},{6,7},{7,8},{8,9},{9,10},{10,1... | collective-permute-start | bytes 393224 | tf_op jit(solution)/shard_map/ppermute | solution.py:132
  70.6 1.1 copy-start.10
  71.7 1.1 copy-start.18
  72.9 12.1 %copy-start.1 = (f32[768,256]{1,0:T(8,128)S(1)}, f32[768,256]{1,0:T(8,128)}, u32[]{:S(2)}) copy-start(f32[768,256]{1,0:T(8,128)} %copy-done) | copy-start | bytes 2359300
  73.5 12.6 %copy-start.11 = (f32[768,256]{1,0:T(8,128)}, f32[768,256]{1,0:T(8,128)S(1)}, u32[]{:S(2)}) copy-start(f32[768,256]{1,0:T(8,128)S(1)} %get-tuple-element.54.refs_1_) | copy-start | bytes 2359300
  73.5 12.6 %collective-permute-start.5 = (f32[128,256]{1,0:T(8,128)S(1)}, f32[128,256]{1,0:T(8,128)S(1)}, u32[]{:S(2)}, u32[]{:S(2)}) collective-permute-start(f32[128,256]{1,0:T(8,128)S(1)} %get-tuple-element.51), channel_id=1, source_target_pairs={{16,0},{32,16},{48,32},{64,48},{80,64},{96,80},{112,96},{128,112},... | collective-permute-start | bytes 393224 | tf_op jit(solution)/shard_map/ppermute | solution.py:132
  77.5 8.6 %collective-permute-start.4 = (f32[128,256]{1,0:T(8,128)S(1)}, f32[128,256]{1,0:T(8,128)S(1)}, u32[]{:S(2)}, u32[]{:S(2)}) collective-permute-start(f32[128,256]{1,0:T(8,128)S(1)} %get-tuple-element.51), channel_id=1, source_target_pairs={{0,16},{16,32},{32,48},{48,64},{64,80},{80,96},{96,112},{112,128},... | collective-permute-start | bytes 393224 | tf_op jit(solution)/shard_map/ppermute | solution.py:132
  79.7 6.7 %collective-permute-start.7 = (f32[128,256]{1,0:T(8,128)S(1)}, f32[128,256]{1,0:T(8,128)S(1)}, u32[]{:S(2)}, u32[]{:S(2)}) collective-permute-start(f32[128,256]{1,0:T(8,128)S(1)} %get-tuple-element.52), channel_id=1, source_target_pairs={{1,0},{2,1},{3,2},{4,3},{5,4},{6,5},{7,6},{8,7},{9,8},{10,9},{11,1... | collective-permute-start | bytes 393224 | tf_op jit(solution)/shard_map/ppermute | solution.py:132
  81.0 6.3 %collective-permute-start.6 = (f32[128,256]{1,0:T(8,128)S(1)}, f32[128,256]{1,0:T(8,128)S(1)}, u32[]{:S(2)}, u32[]{:S(2)}) collective-permute-start(f32[128,256]{1,0:T(8,128)S(1)} %get-tuple-element.52), channel_id=1, source_target_pairs={{0,1},{1,2},{2,3},{3,4},{4,5},{5,6},{6,7},{7,8},{8,9},{9,10},{10,1... | collective-permute-start | bytes 393224 | tf_op jit(solution)/shard_map/ppermute | solution.py:132
  119.9 1.1 copy-start.12
  122.1 12.1 %copy-start.2 = (f32[768,256]{1,0:T(8,128)S(1)}, f32[768,256]{1,0:T(8,128)}, u32[]{:S(2)}) copy-start(f32[768,256]{1,0:T(8,128)} %copy-done) | copy-start | bytes 2359300
  122.8 12.6 %copy-start.13 = (f32[768,256]{1,0:T(8,128)}, f32[768,256]{1,0:T(8,128)S(1)}, u32[]{:S(2)}) copy-start(f32[768,256]{1,0:T(8,128)S(1)} %get-tuple-element.61.refs_1_) | copy-start | bytes 2359300
  122.8 12.6 %collective-permute-start.9 = (f32[128,256]{1,0:T(8,128)S(1)}, f32[128,256]{1,0:T(8,128)S(1)}, u32[]{:S(2)}, u32[]{:S(2)}) collective-permute-start(f32[128,256]{1,0:T(8,128)S(1)} %get-tuple-element.58), channel_id=1, source_target_pairs={{16,0},{32,16},{48,32},{64,48},{80,64},{96,80},{112,96},{128,112},... | collective-permute-start | bytes 393224 | tf_op jit(solution)/shard_map/ppermute | solution.py:132
  126.8 8.6 %collective-permute-start.8 = (f32[128,256]{1,0:T(8,128)S(1)}, f32[128,256]{1,0:T(8,128)S(1)}, u32[]{:S(2)}, u32[]{:S(2)}) collective-permute-start(f32[128,256]{1,0:T(8,128)S(1)} %get-tuple-element.58), channel_id=1, source_target_pairs={{0,16},{16,32},{32,48},{48,64},{64,80},{80,96},{96,112},{112,128},... | collective-permute-start | bytes 393224 | tf_op jit(solution)/shard_map/ppermute | solution.py:132
  129.0 6.7 %collective-permute-start.11 = (f32[128,256]{1,0:T(8,128)S(1)}, f32[128,256]{1,0:T(8,128)S(1)}, u32[]{:S(2)}, u32[]{:S(2)}) collective-permute-start(f32[128,256]{1,0:T(8,128)S(1)} %get-tuple-element.59), channel_id=1, source_target_pairs={{1,0},{2,1},{3,2},{4,3},{5,4},{6,5},{7,6},{8,7},{9,8},{10,9},{11,1... | collective-permute-start | bytes 393224 | tf_op jit(solution)/shard_map/ppermute | solution.py:132
  130.3 6.3 %collective-permute-start.10 = (f32[128,256]{1,0:T(8,128)S(1)}, f32[128,256]{1,0:T(8,128)S(1)}, u32[]{:S(2)}, u32[]{:S(2)}) collective-permute-start(f32[128,256]{1,0:T(8,128)S(1)} %get-tuple-element.59), channel_id=1, source_target_pairs={{0,1},{1,2},{2,3},{3,4},{4,5},{5,6},{6,7},{7,8},{8,9},{9,10},{10,1... | collective-permute-start | bytes 393224 | tf_op jit(solution)/shard_map/ppermute | solution.py:132
  135.4 31.0 %copy-start.14 = (f32[768,256]{1,0:T(8,128)S(1)}, f32[768,256]{1,0:T(8,128)}, u32[]{:S(2)}) copy-start(f32[768,256]{1,0:T(8,128)} %copy-done.13) | copy-start | bytes 2359300
  (11 other events, 9.5 us)

commit v2 on v1

v2 whole, which is shorter than its diff:
```python
import functools

import jax
import jax.numpy as jnp
from jax import lax
from jax.experimental import pallas as pl
from jax.experimental.pallas import tpu as pltpu
from jax.sharding import Mesh
from jax.sharding import PartitionSpec as P

ORDER = 768
FSLOT = 128
COLS = 256
ITERS = 3
CHUNKS = ORDER // COLS
GX = ("z", "c")
GY = ("y", "x")
NEAR = ("c", "y", "x")
FAR = ("z",)

step_length = 0.5
epsilon = 1e-06

f32 = jnp.float32
bf16 = jnp.bfloat16


def dot(a, b):
    return lax.dot_general(a, b, (((1,), (0,)), ((), ())), preferred_element_type=f32)


def split(x):
    high = x.astype(bf16)
    return high, (x - high.astype(f32)).astype(bf16)


def product(a_high, a_low, m_high, m_low):
    return dot(a_high, m_high) + (dot(a_high, m_low) + dot(a_low, m_high))


def live_rows(order, columns):
    return lax.broadcasted_iota(jnp.int32, (ORDER, columns), 0) < order


def chunk(number):
    return slice(number * COLS, (number + 1) * COLS)


def chunk_copies(source, target, sems):
    copies = [
        pltpu.make_async_copy(source.at[pl.ds(number * COLS, COLS), :], target.at[pl.ds(number * COLS, COLS), :], sems.at[number])
        for number in range(CHUNKS)
    ]
    for copy in copies:
        copy.start()
    return copies


def first_kernel(place, orders, operator, warm, face_x, face_y, contact,
                 faces_high_out, faces_low_out, slots_out, floor_out, m_out, m_high_out, m_low_out, near_x_out, near_y_out,
                 rows_here, sems):
    copies = chunk_copies(operator, rows_here, sems)
    order = orders[place[1], place[0]]
    m = jnp.where(live_rows(order, COLS), warm[...].T, 0.0)
    m_out[...] = m
    m_high, m_low = split(m)
    m_high_out[...] = m_high
    m_low_out[...] = m_low
    floor = jnp.where(contact[...] == 1, 0.0, -jnp.inf)
    floor_out[...] = jnp.broadcast_to(floor, (FSLOT, ORDER)).T.astype(bf16)
    slots_out[0:1, :] = face_x[...]
    slots_out[1:2, :] = face_y[...]
    column = jnp.concatenate([jnp.broadcast_to(face[...].astype(f32), (FSLOT, FSLOT)).T for face in (face_x, face_y)], axis=0)
    wide = jnp.concatenate([column] * (COLS // FSLOT), axis=1)
    lanes = lax.broadcasted_iota(jnp.int32, (2 * FSLOT, COLS), 1)
    face_high = jnp.zeros((2 * FSLOT, ORDER), f32)
    face_low = jnp.zeros((2 * FSLOT, ORDER), f32)
    for number, copy in enumerate(copies):
        pick = jnp.where(wide == (lanes + number * COLS).astype(f32), 1.0, 0.0).astype(bf16)
        copy.wait()
        high, low = split(rows_here[chunk(number), :])
        face_high += dot(pick, high)
        face_low += dot(pick, low)
    face_high = face_high.astype(bf16)
    face_low = face_low.astype(bf16)
    faces_high_out[...] = face_high
    faces_low_out[...] = face_low
    near = product(face_high, face_low, m_high, m_low)
    near_x_out[...] = near[:FSLOT]
    near_y_out[...] = near[FSLOT:]


def main_kernel(place, orders, operator, loads, m_high, m_low, local_out, rows_here, loads_here, sems, loads_sem):
    copies = chunk_copies(operator, rows_here, sems)
    loads_copy = pltpu.make_async_copy(loads, loads_here, loads_sem)
    loads_copy.start()
    order = orders[place[1], place[0]]
    for number, copy in enumerate(copies):
        copy.wait()
        high, low = split(rows_here[chunk(number), :])
        local_out[chunk(number), :] = product(high, low, m_high[...], m_low[...])
    loads_copy.wait()
    live = live_rows(order, COLS)
    local_out[...] = jnp.where(live, local_out[...] - loads_here[...].T, 0.0)


def gradient_kernel(slots, local, left, right, below, above, gradient_out, squares_out):
    rows = lax.broadcasted_iota(jnp.int32, (ORDER, FSLOT), 0)
    spots = jnp.concatenate([jnp.where(rows == slots[number : number + 1, :], 1.0, 0.0).astype(bf16) for number in range(2)], axis=1)
    sums = jnp.concatenate([left[...] + right[...], below[...] + above[...]], axis=0)
    sum_high, sum_low = split(sums)
    gradient = local[...] - (dot(spots, sum_high) + dot(spots, sum_low))
    gradient_out[...] = gradient
    squares_out[...] = jnp.sum(gradient * gradient, axis=0, keepdims=True)


def updated(everything, m, gradient, floor, count):
    squares = jnp.sum(everything[...], axis=0)
    rate = step_length / jnp.sqrt(squares / count + epsilon)
    lowest = jnp.concatenate([floor[...].astype(f32)] * (COLS // FSLOT), axis=1)
    return jnp.maximum(m[...] - gradient[...] * rate, lowest)


def update_kernel(count, everything, m, gradient, floor, faces_high, faces_low, m_out, m_high_out, m_low_out, near_x_out, near_y_out):
    new = updated(everything, m, gradient, floor, count)
    m_out[...] = new
    m_high, m_low = split(new)
    m_high_out[...] = m_high
    m_low_out[...] = m_low
    near = product(faces_high[...], faces_low[...], m_high, m_low)
    near_x_out[...] = near[:FSLOT]
    near_y_out[...] = near[FSLOT:]


def last_kernel(count, everything, m, gradient, floor, out, out_here, sems):
    squares = jnp.sum(everything[...], axis=0)
    rate = step_length / jnp.sqrt(squares / count + epsilon)
    copies = []
    for number in range(CHUNKS):
        part = chunk(number)
        lowest = jnp.concatenate([floor[part, :].astype(f32)] * (COLS // FSLOT), axis=1)
        out_here[:, part] = jnp.maximum(m[part, :] - gradient[part, :] * rate, lowest).T
        where = pl.ds(number * COLS, COLS)
        copies.append(pltpu.make_async_copy(out_here.at[:, where], out.at[:, where], sems.at[number]))
        copies[-1].start()
    for copy in copies:
        copy.wait()


HERE = pl.BlockSpec(memory_space=pltpu.VMEM)
SMEM = pl.BlockSpec(memory_space=pltpu.SMEM)
ANY = pl.BlockSpec(memory_space=pl.ANY)


def outside(x):
    return pltpu.with_memory_space_constraint(x, pltpu.HBM)


def scalar(x):
    return x, SMEM


def far(x):
    return outside(x), ANY


def loaded(x):
    return outside(x), HERE


def kept(x):
    return pltpu.with_memory_space_constraint(x, pltpu.VMEM), HERE


def keep(shape, dtype):
    return pltpu.VMEM(shape, dtype), HERE


def call(kernel, name, outs, args, scratch=()):
    return pl.pallas_call(
        kernel,
        name=name,
        out_shape=tuple(shape for shape, _ in outs),
        in_specs=[spec for _, spec in args],
        out_specs=tuple(spec for _, spec in outs),
        scratch_shapes=list(scratch),
        compiler_params=pltpu.CompilerParams(vmem_limit_bytes=24 * 2**20),
    )(*(arg for arg, _ in args))


def passed_along(block, axis, distance):
    devices = range(lax.axis_size(axis))
    route = [(i - distance, i) for i in devices if i - distance in devices]
    return lax.ppermute(block, axis, route)


def from_everyone(x, axis):
    copies = jnp.broadcast_to(x[None], (lax.axis_size(axis), *x.shape))
    return lax.all_to_all(copies, axis, split_axis=0, concat_axis=0, tiled=True)


def body(operator, loads, warm, orders, face_x, face_y, contact):
    count = float(lax.axis_size(GX) * lax.axis_size(GY) * ORDER)
    place = jnp.stack([lax.axis_index(GX), lax.axis_index(GY)]).astype(jnp.int32)
    here = [scalar(place), scalar(outside(orders.T))]
    faces = keep((2 * FSLOT, ORDER), bf16)
    state = keep((ORDER, COLS), f32)
    half = keep((ORDER, COLS), bf16)
    face = keep((FSLOT, COLS), f32)
    rows_here = pltpu.VMEM((ORDER, ORDER), f32)
    loads_here = pltpu.VMEM((COLS, ORDER), f32)
    sems = pltpu.SemaphoreType.DMA((CHUNKS,))
    faces_high, faces_low, slots, floor, m, m_high, m_low, near_x, near_y = call(
        first_kernel, "first",
        [faces, faces, keep((2, FSLOT), jnp.int32), keep((ORDER, FSLOT), bf16), state, half, half, face, face],
        [*here, far(operator[0, 0]), loaded(warm[0, 0]), loaded(face_x[0]), loaded(face_y[0]), loaded(contact[0])],
        [rows_here, sems],
    )
    for iteration in range(ITERS):
        below = passed_along(near_y, GY, 1)
        above = passed_along(near_y, GY, -1)
        left = passed_along(near_x, GX, 1)
        right = passed_along(near_x, GX, -1)
        (local,) = call(
            main_kernel, "main", [state],
            [*here, far(operator[0, 0]), far(loads[0, 0]), kept(m_high), kept(m_low)],
            [rows_here, loads_here, sems, pltpu.SemaphoreType.DMA],
        )
        gradient, squares = call(
            gradient_kernel, "gradient", [state, keep((1, COLS), f32)],
            [kept(x) for x in (slots, local, left, right, below, above)],
        )
        squares = jnp.sum(from_everyone(squares, NEAR), axis=0)
        everything = from_everyone(squares, FAR)
        given = [kept(x) for x in (everything, m, gradient, floor)]
        if iteration < ITERS - 1:
            m, m_high, m_low, near_x, near_y = call(
                functools.partial(update_kernel, count), "update", [state, half, half, face, face],
                [*given, kept(faces_high), kept(faces_low)],
            )
        else:
            (out,) = call(
                functools.partial(last_kernel, count), "last",
                [(pltpu.HBM((COLS, ORDER), f32), ANY)], given, [loads_here, sems],
            )
    return out[None, None]


def solution(mesh):
    shape = dict(mesh.shape)
    finer = Mesh(mesh.devices.reshape(shape["gx"] // 2, 2, 4, shape["gy"] // 4), ("z", "c", "y", "x"))
    in_specs = (
        P(GX, GY, None, None),
        P(GX, GY, None, None),
        P(GX, GY, None, None),
        P(),
        P(GX, GY, None),
        P(GX, GY, None),
        P(GX, GY, None),
    )
    out_specs = P(GX, GY, None, None)
    return jax.shard_map(body, mesh=finer, in_specs=in_specs, out_specs=out_specs, check_vma=False)
```

time: 169 us -> 153 us (0.905)
  local copies, waits for them, and re-layouts: 16.7 us -> 0.1 us
  Pallas kernels: 9.18 us -> 20.7 us
  blocking collectives: 98.4 us -> 92.5 us
  waiting for transfers between devices: 2.4 us -> 0.03 us
    unnamed x47 -> x0, local copies, waits for them, and re-layouts: 16.6 us -> none
    pallas_call x10, Pallas kernels: 9.18 us -> 20.7 us  [call(): pl.pallas_call(kernel, name=name, out_shape=tuple((shape for shape, _ in...]
    all_to_all x6, blocking collectives: 98.4 us -> 92.5 us  [from_everyone(): return lax.all_to_all(copies, axis, split_axis=0, concat_axis=0, tiled=True)]
    ppermute x12, waiting for transfers between devices: 2.4 us -> 0.03 us  [passed_along(): return lax.ppermute(block, axis, route)]
  transfers between devices with their start and end apart: 12 -> 12, of which waited for: 4 -> 0; matrix products, arithmetic and copies ran while one was open for 0% -> 0% of each run, Pallas kernels for 2% -> 8%
where the time goes in v2:
time: 153 us
  blocking collectives  92.5 us (60%)
  starting transfers between devices  38.8 us (25%)
  Pallas kernels  20.7 us (14%)
    all_to_all x6, blocking collectives, from_everyone(): return lax.all_to_all(copies, axis, split_axis=0, concat_axis=0, tiled=True)  92.5 us
    ppermute x12, starting transfers between devices, passed_along(): return lax.ppermute(block, axis, route)  38.8 us
    pallas_call x10, Pallas kernels, call(): pl.pallas_call(kernel, name=name, out_shape=tuple((shape for shape, _ in...  20.7 us
  transfers between devices with their start and end apart: 12, of which 0 were waited for; matrix products, arithmetic and copies ran while one was open for 0% of the time, Pallas kernels for 8%

profile of v2, /device:TPU:1, one launch (start us, length us, event | category | flops | bytes accessed | tf_op | source)
XLA Modules:
  0.0 152.7 jit_solution(5619753788699277111)
XLA Ops:
  0.1 4.3 %first.1 = (bf16[256,768]{1,0:T(8,128)(2,1)S(1)}, bf16[256,768]{1,0:T(8,128)(2,1)S(1)}, s32[2,128]{1,0:T(2,128)S(1)}, bf16[768,128]{1,0:T(8,128)(2,1)S(1)}, f32[...) custom-call(s32[2]{0:T(128)S(1)} %pad_add_fusion.place, ...), custom_call_target="tpu_custom_call" | custom-call | tf_op jit(solution)/shard_map/first/pallas_call | solution.py:180
  4.4 8.7 %collective-permute-start.1 = (f32[128,256]{1,0:T(8,128)S(1)}, f32[128,256]{1,0:T(8,128)S(1)}, u32[]{:S(2)}, u32[]{:S(2)}) collective-permute-start(f32[128,256]{1,0:T(8,128)S(1)} %get-tuple-element.33), channel_id=1, source_target_pairs={{16,0},{32,16},{48,32},{64,48},{80,64},{96,80},{112,96},{128,112},... | collective-permute-start | bytes 393224 | tf_op jit(solution)/shard_map/ppermute | solution.py:194
  13.1 1.9 %collective-permute-start = (f32[128,256]{1,0:T(8,128)S(1)}, f32[128,256]{1,0:T(8,128)S(1)}, u32[]{:S(2)}, u32[]{:S(2)}) collective-permute-start(f32[128,256]{1,0:T(8,128)S(1)} %get-tuple-element.33), channel_id=1, source_target_pairs={{0,16},{16,32},{32,48},{48,64},{64,80},{80,96},{96,112},{112,128},... | collective-permute-start | bytes 393224 | tf_op jit(solution)/shard_map/ppermute | solution.py:194
  15.1 1.3 collective-permute-start.3
  16.4 4.0 %collective-permute-start.2 = (f32[128,256]{1,0:T(8,128)S(1)}, f32[128,256]{1,0:T(8,128)S(1)}, u32[]{:S(2)}, u32[]{:S(2)}) collective-permute-start(f32[128,256]{1,0:T(8,128)S(1)} %get-tuple-element.34), channel_id=1, source_target_pairs={{0,1},{1,2},{2,3},{3,4},{4,5},{5,6},{6,7},{7,8},{8,9},{9,10},{10,1... | collective-permute-start | bytes 393224 | tf_op jit(solution)/shard_map/ppermute | solution.py:194
  20.4 4.3 %main.3.local = f32[768,256]{1,0:T(8,128)S(1)} custom-call(s32[2]{0:T(128)S(1)} %pad_add_fusion.place, s32[16,32]{1,0:T(8,128)} %bitcast.25, f32[768,768]{1,0:T(8,128)} %bitcast.17, f32[256,768]{1,0:T(8,128)} %bitcast.20, bf16[768,256]{1,0:T(8,128)(2,1)S(1)} %get-tuple-element.31.m_high, bf16[768,256]{1,0:T(8,128)(2,1)S(1)} %get-tuple-element.32.m_low), custom_call_target="tpu_custom_call" | custom-call | tf_op jit(solution)/shard_map/main/pallas_call | solution.py:180
  25.1 12.0 %all_to_all.30 = f32[32,1,256]{2,1,0:T(1,128)S(1)} all-to-all(f32[32,1,256]{2,1,0:T(1,128)S(1)} %broadcast_in_dim.21), channel_id=1, replica_groups=mesh['z'=16,'c'=2,'y'=4,'x'=4] {'c','y','x'}, dimensions={0} | all-to-all | bytes 65536 | tf_op jit(solution)/shard_map/all_to_all | solution.py:199
  37.2 25.9 %all_to_all.31.everything = f32[16,1,256]{2,1,0:T(1,128)S(1)} all-to-all(f32[16,1,256]{2,1,0:T(1,128)S(1)} %broadcast_in_dim.22), channel_id=1, replica_groups=mesh['z'=16,'c'=2,'y'=4,'x'=4] {'z'}, dimensions={0} | all-to-all | bytes 32768 | tf_op jit(solution)/shard_map/all_to_all | solution.py:199
  63.1 0.6 update.2
  63.8 3.9 %collective-permute-start.5 = (f32[128,256]{1,0:T(8,128)S(1)}, f32[128,256]{1,0:T(8,128)S(1)}, u32[]{:S(2)}, u32[]{:S(2)}) collective-permute-start(f32[128,256]{1,0:T(8,128)S(1)} %get-tuple-element.43), channel_id=1, source_target_pairs={{16,0},{32,16},{48,32},{64,48},{80,64},{96,80},{112,96},{128,112},... | collective-permute-start | bytes 393224 | tf_op jit(solution)/shard_map/ppermute | solution.py:194
  67.7 2.2 %collective-permute-start.4 = (f32[128,256]{1,0:T(8,128)S(1)}, f32[128,256]{1,0:T(8,128)S(1)}, u32[]{:S(2)}, u32[]{:S(2)}) collective-permute-start(f32[128,256]{1,0:T(8,128)S(1)} %get-tuple-element.43), channel_id=1, source_target_pairs={{0,16},{16,32},{32,48},{48,64},{64,80},{80,96},{96,112},{112,128},... | collective-permute-start | bytes 393224 | tf_op jit(solution)/shard_map/ppermute | solution.py:194
  69.9 1.3 collective-permute-start.7
  71.2 4.0 %collective-permute-start.6 = (f32[128,256]{1,0:T(8,128)S(1)}, f32[128,256]{1,0:T(8,128)S(1)}, u32[]{:S(2)}, u32[]{:S(2)}) collective-permute-start(f32[128,256]{1,0:T(8,128)S(1)} %get-tuple-element.44), channel_id=1, source_target_pairs={{0,1},{1,2},{2,3},{3,4},{4,5},{5,6},{6,7},{7,8},{8,9},{9,10},{10,1... | collective-permute-start | bytes 393224 | tf_op jit(solution)/shard_map/ppermute | solution.py:194
  75.2 4.3 %main.4.local = f32[768,256]{1,0:T(8,128)S(1)} custom-call(s32[2]{0:T(128)S(1)} %pad_add_fusion.place, s32[16,32]{1,0:T(8,128)} %bitcast.26, f32[768,768]{1,0:T(8,128)} %bitcast.18, f32[256,768]{1,0:T(8,128)} %bitcast.21, bf16[768,256]{1,0:T(8,128)(2,1)S(1)} %get-tuple-element.41.m_high, bf16[768,256]{1,0:T(8,128)(2,1)S(1)} %get-tuple-element.42.m_low), custom_call_target="tpu_custom_call" | custom-call | tf_op jit(solution)/shard_map/main/pallas_call | solution.py:180
  80.0 13.5 %all_to_all.32 = f32[32,1,256]{2,1,0:T(1,128)S(1)} all-to-all(f32[32,1,256]{2,1,0:T(1,128)S(1)} %broadcast_in_dim.24), channel_id=1, replica_groups=mesh['z'=16,'c'=2,'y'=4,'x'=4] {'c','y','x'}, dimensions={0} | all-to-all | bytes 65536 | tf_op jit(solution)/shard_map/all_to_all | solution.py:199
  93.5 13.8 %all_to_all.33.everything = f32[16,1,256]{2,1,0:T(1,128)S(1)} all-to-all(f32[16,1,256]{2,1,0:T(1,128)S(1)} %broadcast_in_dim.50), channel_id=1, replica_groups=mesh['z'=16,'c'=2,'y'=4,'x'=4] {'z'}, dimensions={0} | all-to-all | bytes 32768 | tf_op jit(solution)/shard_map/all_to_all | solution.py:199
  108.0 4.0 %collective-permute-start.9 = (f32[128,256]{1,0:T(8,128)S(1)}, f32[128,256]{1,0:T(8,128)S(1)}, u32[]{:S(2)}, u32[]{:S(2)}) collective-permute-start(f32[128,256]{1,0:T(8,128)S(1)} %get-tuple-element.50), channel_id=1, source_target_pairs={{16,0},{32,16},{48,32},{64,48},{80,64},{96,80},{112,96},{128,112},... | collective-permute-start | bytes 393224 | tf_op jit(solution)/shard_map/ppermute | solution.py:194
  112.0 2.2 %collective-permute-start.8 = (f32[128,256]{1,0:T(8,128)S(1)}, f32[128,256]{1,0:T(8,128)S(1)}, u32[]{:S(2)}, u32[]{:S(2)}) collective-permute-start(f32[128,256]{1,0:T(8,128)S(1)} %get-tuple-element.50), channel_id=1, source_target_pairs={{0,16},{16,32},{32,48},{48,64},{64,80},{80,96},{96,112},{112,128},... | collective-permute-start | bytes 393224 | tf_op jit(solution)/shard_map/ppermute | solution.py:194
  114.2 1.3 collective-permute-start.11
  115.5 4.0 %collective-permute-start.10 = (f32[128,256]{1,0:T(8,128)S(1)}, f32[128,256]{1,0:T(8,128)S(1)}, u32[]{:S(2)}, u32[]{:S(2)}) collective-permute-start(f32[128,256]{1,0:T(8,128)S(1)} %get-tuple-element.51), channel_id=1, source_target_pairs={{0,1},{1,2},{2,3},{3,4},{4,5},{5,6},{6,7},{7,8},{8,9},{9,10},{10,1... | collective-permute-start | bytes 393224 | tf_op jit(solution)/shard_map/ppermute | solution.py:194
  119.5 4.3 %main.5.local = f32[768,256]{1,0:T(8,128)S(1)} custom-call(s32[2]{0:T(128)S(1)} %pad_add_fusion.place, s32[16,32]{1,0:T(8,128)} %bitcast.27, f32[768,768]{1,0:T(8,128)} %bitcast.19, f32[256,768]{1,0:T(8,128)} %bitcast.22, bf16[768,256]{1,0:T(8,128)(2,1)S(1)} %get-tuple-element.48.m_high, bf16[768,256]{1,0:T(8,128)(2,1)S(1)} %get-tuple-element.49.m_low), custom_call_target="tpu_custom_call" | custom-call | tf_op jit(solution)/shard_map/main/pallas_call | solution.py:180
  124.2 13.5 %all_to_all.34 = f32[32,1,256]{2,1,0:T(1,128)S(1)} all-to-all(f32[32,1,256]{2,1,0:T(1,128)S(1)} %broadcast_in_dim.52), channel_id=1, replica_groups=mesh['z'=16,'c'=2,'y'=4,'x'=4] {'c','y','x'}, dimensions={0} | all-to-all | bytes 65536 | tf_op jit(solution)/shard_map/all_to_all | solution.py:199
  137.8 13.8 %all_to_all.35.everything = f32[16,1,256]{2,1,0:T(1,128)S(1)} all-to-all(f32[16,1,256]{2,1,0:T(1,128)S(1)} %broadcast_in_dim.53), channel_id=1, replica_groups=mesh['z'=16,'c'=2,'y'=4,'x'=4] {'z'}, dimensions={0} | all-to-all | bytes 32768 | tf_op jit(solution)/shard_map/all_to_all | solution.py:199
  151.6 1.1 last.1
  (26 shorter events, 2.1 us)
Async XLA Ops:
  4.4 20.3 %collective-permute-start.1 = (f32[128,256]{1,0:T(8,128)S(1)}, f32[128,256]{1,0:T(8,128)S(1)}, u32[]{:S(2)}, u32[]{:S(2)}) collective-permute-start(f32[128,256]{1,0:T(8,128)S(1)} %get-tuple-element.33), channel_id=1, source_target_pairs={{16,0},{32,16},{48,32},{64,48},{80,64},{96,80},{112,96},{128,112},... | collective-permute-start | bytes 393224 | tf_op jit(solution)/shard_map/ppermute | solution.py:194
  13.1 11.5 %collective-permute-start = (f32[128,256]{1,0:T(8,128)S(1)}, f32[128,256]{1,0:T(8,128)S(1)}, u32[]{:S(2)}, u32[]{:S(2)}) collective-permute-start(f32[128,256]{1,0:T(8,128)S(1)} %get-tuple-element.33), channel_id=1, source_target_pairs={{0,16},{16,32},{32,48},{48,64},{64,80},{80,96},{96,112},{112,128},... | collective-permute-start | bytes 393224 | tf_op jit(solution)/shard_map/ppermute | solution.py:194
  15.1 9.6 %collective-permute-start.3 = (f32[128,256]{1,0:T(8,128)S(1)}, f32[128,256]{1,0:T(8,128)S(1)}, u32[]{:S(2)}, u32[]{:S(2)}) collective-permute-start(f32[128,256]{1,0:T(8,128)S(1)} %get-tuple-element.34), channel_id=1, source_target_pairs={{1,0},{2,1},{3,2},{4,3},{5,4},{6,5},{7,6},{8,7},{9,8},{10,9},{11,1... | collective-permute-start | bytes 393224 | tf_op jit(solution)/shard_map/ppermute | solution.py:194
  16.4 8.3 %collective-permute-start.2 = (f32[128,256]{1,0:T(8,128)S(1)}, f32[128,256]{1,0:T(8,128)S(1)}, u32[]{:S(2)}, u32[]{:S(2)}) collective-permute-start(f32[128,256]{1,0:T(8,128)S(1)} %get-tuple-element.34), channel_id=1, source_target_pairs={{0,1},{1,2},{2,3},{3,4},{4,5},{5,6},{6,7},{7,8},{8,9},{9,10},{10,1... | collective-permute-start | bytes 393224 | tf_op jit(solution)/shard_map/ppermute | solution.py:194
  63.8 15.8 %collective-permute-start.5 = (f32[128,256]{1,0:T(8,128)S(1)}, f32[128,256]{1,0:T(8,128)S(1)}, u32[]{:S(2)}, u32[]{:S(2)}) collective-permute-start(f32[128,256]{1,0:T(8,128)S(1)} %get-tuple-element.43), channel_id=1, source_target_pairs={{16,0},{32,16},{48,32},{64,48},{80,64},{96,80},{112,96},{128,112},... | collective-permute-start | bytes 393224 | tf_op jit(solution)/shard_map/ppermute | solution.py:194
  67.7 11.8 %collective-permute-start.4 = (f32[128,256]{1,0:T(8,128)S(1)}, f32[128,256]{1,0:T(8,128)S(1)}, u32[]{:S(2)}, u32[]{:S(2)}) collective-permute-start(f32[128,256]{1,0:T(8,128)S(1)} %get-tuple-element.43), channel_id=1, source_target_pairs={{0,16},{16,32},{32,48},{48,64},{64,80},{80,96},{96,112},{112,128},... | collective-permute-start | bytes 393224 | tf_op jit(solution)/shard_map/ppermute | solution.py:194
  69.9 9.6 %collective-permute-start.7 = (f32[128,256]{1,0:T(8,128)S(1)}, f32[128,256]{1,0:T(8,128)S(1)}, u32[]{:S(2)}, u32[]{:S(2)}) collective-permute-start(f32[128,256]{1,0:T(8,128)S(1)} %get-tuple-element.44), channel_id=1, source_target_pairs={{1,0},{2,1},{3,2},{4,3},{5,4},{6,5},{7,6},{8,7},{9,8},{10,9},{11,1... | collective-permute-start | bytes 393224 | tf_op jit(solution)/shard_map/ppermute | solution.py:194
  71.2 8.3 %collective-permute-start.6 = (f32[128,256]{1,0:T(8,128)S(1)}, f32[128,256]{1,0:T(8,128)S(1)}, u32[]{:S(2)}, u32[]{:S(2)}) collective-permute-start(f32[128,256]{1,0:T(8,128)S(1)} %get-tuple-element.44), channel_id=1, source_target_pairs={{0,1},{1,2},{2,3},{3,4},{4,5},{5,6},{6,7},{7,8},{8,9},{9,10},{10,1... | collective-permute-start | bytes 393224 | tf_op jit(solution)/shard_map/ppermute | solution.py:194
  108.0 15.8 %collective-permute-start.9 = (f32[128,256]{1,0:T(8,128)S(1)}, f32[128,256]{1,0:T(8,128)S(1)}, u32[]{:S(2)}, u32[]{:S(2)}) collective-permute-start(f32[128,256]{1,0:T(8,128)S(1)} %get-tuple-element.50), channel_id=1, source_target_pairs={{16,0},{32,16},{48,32},{64,48},{80,64},{96,80},{112,96},{128,112},... | collective-permute-start | bytes 393224 | tf_op jit(solution)/shard_map/ppermute | solution.py:194
  112.0 11.8 %collective-permute-start.8 = (f32[128,256]{1,0:T(8,128)S(1)}, f32[128,256]{1,0:T(8,128)S(1)}, u32[]{:S(2)}, u32[]{:S(2)}) collective-permute-start(f32[128,256]{1,0:T(8,128)S(1)} %get-tuple-element.50), channel_id=1, source_target_pairs={{0,16},{16,32},{32,48},{48,64},{64,80},{80,96},{96,112},{112,128},... | collective-permute-start | bytes 393224 | tf_op jit(solution)/shard_map/ppermute | solution.py:194
  114.2 9.6 %collective-permute-start.11 = (f32[128,256]{1,0:T(8,128)S(1)}, f32[128,256]{1,0:T(8,128)S(1)}, u32[]{:S(2)}, u32[]{:S(2)}) collective-permute-start(f32[128,256]{1,0:T(8,128)S(1)} %get-tuple-element.51), channel_id=1, source_target_pairs={{1,0},{2,1},{3,2},{4,3},{5,4},{6,5},{7,6},{8,7},{9,8},{10,9},{11,1... | collective-permute-start | bytes 393224 | tf_op jit(solution)/shard_map/ppermute | solution.py:194
  115.5 8.3 %collective-permute-start.10 = (f32[128,256]{1,0:T(8,128)S(1)}, f32[128,256]{1,0:T(8,128)S(1)}, u32[]{:S(2)}, u32[]{:S(2)}) collective-permute-start(f32[128,256]{1,0:T(8,128)S(1)} %get-tuple-element.51), channel_id=1, source_target_pairs={{0,1},{1,2},{2,3},{3,4},{4,5},{5,6},{6,7},{7,8},{8,9},{9,10},{10,1... | collective-permute-start | bytes 393224 | tf_op jit(solution)/shard_map/ppermute | solution.py:194

commit v3 on v2

v3 whole, which is shorter than its diff:
```python
import functools

import jax
import jax.numpy as jnp
from jax import lax
from jax.experimental import pallas as pl
from jax.experimental.pallas import tpu as pltpu
from jax.sharding import Mesh
from jax.sharding import PartitionSpec as P

ORDER = 768
FSLOT = 128
COLS = 256
ITERS = 3
CHUNKS = ORDER // COLS
GX = ("z", "c")
GY = ("y", "x")
NEAR = ("c", "y", "x")
FAR = ("z",)

step_length = 0.5
epsilon = 1e-06

f32 = jnp.float32
bf16 = jnp.bfloat16


def dot(a, b):
    return lax.dot_general(a, b, (((1,), (0,)), ((), ())), preferred_element_type=f32)


def split(x):
    high = x.astype(bf16)
    return high, (x - high.astype(f32)).astype(bf16)


def product(a_high, a_low, m_high, m_low):
    return dot(a_high, m_high) + (dot(a_high, m_low) + dot(a_low, m_high))


def live_rows(order, columns):
    return lax.broadcasted_iota(jnp.int32, (ORDER, columns), 0) < order


def chunk(number):
    return slice(number * COLS, (number + 1) * COLS)


def chunk_copies(source, target, sems):
    copies = [
        pltpu.make_async_copy(source.at[:, pl.ds(number * COLS, COLS)], target.at[:, pl.ds(number * COLS, COLS)], sems.at[number])
        for number in range(CHUNKS)
    ]
    for copy in copies:
        copy.start()
    return copies


def first_kernel(orders, operator, warm, face_x, face_y, contact,
                 high_out, low_out, faces_high_out, faces_low_out, slots_out, floor_out, m_out, m_high_out, m_low_out, near_x_out, near_y_out,
                 orders_here, rows_here, warm_here, contact_here, sems, small_sems):
    small = [
        pltpu.make_async_copy(face_x, slots_out.at[0:1, :], small_sems.at[0]),
        pltpu.make_async_copy(face_y, slots_out.at[1:2, :], small_sems.at[1]),
        pltpu.make_async_copy(orders, orders_here, small_sems.at[2]),
        pltpu.make_async_copy(warm, warm_here, small_sems.at[3]),
        pltpu.make_async_copy(contact, contact_here, small_sems.at[4]),
    ]
    for copy in small:
        copy.start()
    copies = chunk_copies(operator, rows_here, sems)
    small[0].wait()
    small[1].wait()
    column = jnp.concatenate([jnp.broadcast_to(slots_out[n : n + 1, :].astype(f32), (FSLOT, FSLOT)).T for n in range(2)], axis=0)
    wide = jnp.concatenate([column] * (ORDER // FSLOT), axis=1)
    lanes = lax.broadcasted_iota(jnp.int32, (2 * FSLOT, ORDER), 1).astype(f32)
    pick = jnp.where(wide == lanes, 1.0, 0.0).astype(bf16)
    small[4].wait()
    floor = jnp.where(contact_here[...] == 1, 0.0, -jnp.inf)
    floor_out[...] = jnp.broadcast_to(floor, (FSLOT, ORDER)).T.astype(bf16)
    small[2].wait()
    small[3].wait()
    order = order_of(orders_here)
    m = jnp.where(live_rows(order, COLS), warm_here[...].T, 0.0)
    m_out[...] = m
    m_high, m_low = split(m)
    m_high_out[...] = m_high
    m_low_out[...] = m_low
    near = jnp.zeros((2 * FSLOT, COLS), f32)
    for number, copy in enumerate(copies):
        copy.wait()
        part = chunk(number)
        high, low = split(jnp.where(live_rows(order, COLS), rows_here[:, part], 0.0))
        high_out[:, part] = high
        low_out[:, part] = low
        face_high = dot(pick, high).astype(bf16)
        face_low = dot(pick, low).astype(bf16)
        faces_high_out[:, part] = face_high
        faces_low_out[:, part] = face_low
        near += product(face_high, face_low, m_high_out[part, :], m_low_out[part, :])
    near_x_out[...] = near[:FSLOT]
    near_y_out[...] = near[FSLOT:]


def order_of(orders):
    return orders[lax.axis_index(GY), lax.axis_index(GX)]


def first_main_kernel(orders, high, low, m_high, m_low, loads, local_out, rhs_out, orders_here, orders_sem):
    copy = pltpu.make_async_copy(orders, orders_here, orders_sem)
    copy.start()
    total = product(high[...], low[...], m_high[...], m_low[...])
    copy.wait()
    rhs = jnp.where(live_rows(order_of(orders_here), COLS), loads[...].T, 0.0)
    rhs_out[...] = rhs
    local_out[...] = total - rhs


def main_kernel(high, low, m_high, m_low, rhs, local_out):
    local_out[...] = product(high[...], low[...], m_high[...], m_low[...]) - rhs[...]


def middle_kernel(everything, out):
    total = jnp.sum(everything[...], axis=0)
    out[...] = jnp.broadcast_to(total[None], out.shape)


def gradient_kernel(slots, local, outer, inner, below, above, gradient_out, squares_out):
    rows = lax.broadcasted_iota(jnp.int32, (ORDER, FSLOT), 0)
    spots = jnp.concatenate([jnp.where(rows == slots[number : number + 1, :], 1.0, 0.0).astype(bf16) for number in range(2)], axis=1)
    sums = jnp.concatenate([outer[...] + inner[...], below[...] + above[...]], axis=0)
    sum_high, sum_low = split(sums)
    gradient = local[...] - (dot(spots, sum_high) + dot(spots, sum_low))
    gradient_out[...] = gradient
    squares = jnp.sum(gradient * gradient, axis=0, keepdims=True)
    squares_out[...] = jnp.broadcast_to(squares[None], squares_out.shape)


def updated(everything, m, gradient, floor, count):
    squares = jnp.sum(everything[...], axis=0)
    rate = step_length / jnp.sqrt(squares / count + epsilon)
    lowest = jnp.concatenate([floor[...].astype(f32)] * (COLS // FSLOT), axis=1)
    return jnp.maximum(m[...] - gradient[...] * rate, lowest)


def update_kernel(count, everything, m, gradient, floor, faces_high, faces_low, m_out, m_high_out, m_low_out, near_x_out, near_y_out):
    new = updated(everything, m, gradient, floor, count)
    m_out[...] = new
    m_high, m_low = split(new)
    m_high_out[...] = m_high
    m_low_out[...] = m_low
    near = product(faces_high[...], faces_low[...], m_high, m_low)
    near_x_out[...] = near[:FSLOT]
    near_y_out[...] = near[FSLOT:]


def last_kernel(count, everything, m, gradient, floor, out, out_here, sems):
    squares = jnp.sum(everything[...], axis=0)
    rate = step_length / jnp.sqrt(squares / count + epsilon)
    copies = []
    for number in range(CHUNKS):
        part = chunk(number)
        lowest = jnp.concatenate([floor[part, :].astype(f32)] * (COLS // FSLOT), axis=1)
        out_here[:, part] = jnp.maximum(m[part, :] - gradient[part, :] * rate, lowest).T
        where = pl.ds(number * COLS, COLS)
        copies.append(pltpu.make_async_copy(out_here.at[:, where], out.at[:, where], sems.at[number]))
        copies[-1].start()
    for copy in copies:
        copy.wait()


HERE = pl.BlockSpec(memory_space=pltpu.VMEM)
ANY = pl.BlockSpec(memory_space=pl.ANY)


def outside(x):
    return pltpu.with_memory_space_constraint(x, pltpu.HBM)


def far(x):
    return outside(x), ANY


def kept(x):
    return pltpu.with_memory_space_constraint(x, pltpu.VMEM), HERE


def keep(shape, dtype):
    return pltpu.VMEM(shape, dtype), HERE


def call(kernel, outs, args, scratch=()):
    return pl.pallas_call(
        kernel,
        out_shape=tuple(shape for shape, _ in outs),
        in_specs=[spec for _, spec in args],
        out_specs=tuple(spec for _, spec in outs),
        scratch_shapes=list(scratch),
        compiler_params=pltpu.CompilerParams(vmem_limit_bytes=24 * 2**20),
    )(*(arg for arg, _ in args))


def swapped(block, axis, first):
    route = []
    for i in range(first, lax.axis_size(axis) - 1, 2):
        route += [(i, i + 1), (i + 1, i)]
    return lax.ppermute(block, axis, route)


def from_everyone(copies, axis):
    return lax.all_to_all(copies, axis, split_axis=0, concat_axis=0, tiled=True)


def body(operator, loads, warm, orders, face_x, face_y, contact):
    count = float(lax.axis_size(GX) * lax.axis_size(GY) * ORDER)
    orders = orders.T
    square = keep((ORDER, ORDER), bf16)
    faces = keep((2 * FSLOT, ORDER), bf16)
    state = keep((ORDER, COLS), f32)
    half = keep((ORDER, COLS), bf16)
    face = keep((FSLOT, COLS), f32)
    rows_here = pltpu.VMEM((ORDER, ORDER), f32)
    orders_here = pltpu.SMEM(orders.shape, jnp.int32)
    loads_here = pltpu.VMEM((COLS, ORDER), f32)
    sems = pltpu.SemaphoreType.DMA((CHUNKS,))
    high, low, faces_high, faces_low, slots, floor, m, m_high, m_low, near_x, near_y = call(
        first_kernel,
        [square, square, faces, faces, keep((2, FSLOT), jnp.int32), keep((ORDER, FSLOT), bf16), state, half, half, face, face],
        [far(x) for x in (orders, operator[0, 0], warm[0, 0], face_x[0], face_y[0], contact[0])],
        [orders_here, rows_here, loads_here, pltpu.VMEM((1, ORDER), jnp.int32), sems, pltpu.SemaphoreType.DMA((5,))],
    )
    for iteration in range(ITERS):
        below = swapped(near_y, GY, 0)
        above = swapped(near_y, GY, 1)
        outer = swapped(near_x, GX, 1)
        inner = swapped(near_x, GX, 0)
        matrices = [kept(x) for x in (high, low, m_high, m_low)]
        if iteration == 0:
            local, rhs = call(
                first_main_kernel, [state, state], [far(orders), *matrices, kept(loads[0, 0])],
                [orders_here, pltpu.SemaphoreType.DMA],
            )
        else:
            (local,) = call(main_kernel, [state], [*matrices, kept(rhs)])
        gradient, squares = call(
            gradient_kernel, [state, keep((lax.axis_size(NEAR), 1, COLS), f32)],
            [kept(x) for x in (slots, local, outer, inner, below, above)],
        )
        (squares,) = call(
            middle_kernel, [keep((lax.axis_size(FAR), 1, COLS), f32)], [kept(from_everyone(squares, NEAR))]
        )
        everything = from_everyone(squares, FAR)
        given = [kept(x) for x in (everything, m, gradient, floor)]
        if iteration < ITERS - 1:
            m, m_high, m_low, near_x, near_y = call(
                functools.partial(update_kernel, count), [state, half, half, face, face],
                [*given, kept(faces_high), kept(faces_low)],
            )
        else:
            (out,) = call(
                functools.partial(last_kernel, count),
                [(pltpu.HBM((COLS, ORDER), f32), ANY)], given, [loads_here, sems],
            )
    return out[None, None]


def solution(mesh):
    shape = dict(mesh.shape)
    finer = Mesh(mesh.devices.reshape(shape["gx"] // 2, 2, 4, shape["gy"] // 4), ("z", "c", "y", "x"))
    in_specs = (
        P(GX, GY, None, None),
        P(GX, GY, None, None),
        P(GX, GY, None, None),
        P(),
        P(GX, GY, None),
        P(GX, GY, None),
        P(GX, GY, None),
    )
    out_specs = P(GX, GY, None, None)
    return jax.shard_map(body, mesh=finer, in_specs=in_specs, out_specs=out_specs, check_vma=False)
```

time: 153 us -> 152 us (level)
  Pallas kernels: 20.7 us -> 11.9 us
  blocking collectives: 92.5 us -> 98.9 us
  waiting for transfers between devices: 0.03 us -> 5.44 us
  starting transfers between devices: 38.8 us -> 34.5 us
    pallas_call x10 -> x13, Pallas kernels: 20.7 us -> 11.9 us  [call(): pl.pallas_call(kernel, out_shape=tuple((shape for shape, _ in outs)), in_...]
    all_to_all x6, blocking collectives: 92.5 us -> 98.9 us  [from_everyone(): return lax.all_to_all(copies, axis, split_axis=0, concat_axis=0, tiled=True)]
    ppermute x12, waiting for transfers between devices: 0.03 us -> 5.44 us  [swapped(): return lax.ppermute(block, axis, route)]
    ppermute x12, starting transfers between devices: 38.8 us -> 34.5 us  [swapped(): return lax.ppermute(block, axis, route)]
  transfers between devices with their start and end apart: 12 -> 12, of which waited for: 0 -> 3; matrix products, arithmetic and copies ran while one was open for 0% -> 0% of each run, Pallas kernels for 8% -> 3%
where the time goes in v3:
time: 152 us; the launch traced here: 151 us
  blocking collectives  98.9 us (65%)
  starting transfers between devices  34.5 us (23%)
  Pallas kernels  11.9 us (8%)
  waiting for transfers between devices  5.44 us (4%)
    all_to_all x6, blocking collectives, from_everyone(): return lax.all_to_all(copies, axis, split_axis=0, concat_axis=0, tiled=True)  98.9 us
    ppermute x12, starting transfers between devices, swapped(): return lax.ppermute(block, axis, route)  34.5 us
    pallas_call x13, Pallas kernels, call(): pl.pallas_call(kernel, out_shape=tuple((shape for shape, _ in outs)), in_...  11.9 us
    ppermute x12, waiting for transfers between devices, swapped(): return lax.ppermute(block, axis, route)  5.44 us
  transfers between devices with their start and end apart: 12, of which 3 were waited for; matrix products, arithmetic and copies ran while one was open for 0% of the time, Pallas kernels for 3%

profile of v3, /device:TPU:1, one launch (start us, length us, event | category | flops | bytes accessed | tf_op | source)
XLA Modules:
  0.0 151.0 jit_solution(11999340174328621782)
XLA Ops:
  0.0 4.1 %shard_map.73 = (bf16[768,768]{1,0:T(8,128)(2,1)S(1)}, bf16[768,768]{1,0:T(8,128)(2,1)S(1)}, bf16[256,768]{1,0:T(8,128)(2,1)S(1)}, bf16[256,768]{1,0:T(8,128)(2,...) custom-call(s32[16,32]{1,0:T(8,128)} %bitcast.11, ...), custom_call_target="tpu_custom_call" | custom-call | tf_op jit(solution)/shard_map/pallas_call | solution.py:193
  4.1 8.7 %collective-permute-start.1 = (f32[128,256]{1,0:T(8,128)S(1)}, f32[128,256]{1,0:T(8,128)S(1)}, u32[]{:S(2)}, u32[]{:S(2)}) collective-permute-start(f32[128,256]{1,0:T(8,128)S(1)} %get-tuple-element.40), channel_id=1, source_target_pairs={{0,16},{16,0},{32,48},{48,32},{64,80},{80,64},{96,112},{112,96},{1... | collective-permute-start | bytes 393224 | tf_op jit(solution)/shard_map/ppermute | solution.py:207
  12.8 1.9 %collective-permute-start = (f32[128,256]{1,0:T(8,128)S(1)}, f32[128,256]{1,0:T(8,128)S(1)}, u32[]{:S(2)}, u32[]{:S(2)}) collective-permute-start(f32[128,256]{1,0:T(8,128)S(1)} %get-tuple-element.40), channel_id=1, source_target_pairs={{16,32},{32,16},{48,64},{64,48},{80,96},{96,80},{112,128},{128,112... | collective-permute-start | bytes 393224 | tf_op jit(solution)/shard_map/ppermute | solution.py:207
  15.4 1.9 %collective-permute-start.2 = (f32[128,256]{1,0:T(8,128)S(1)}, f32[128,256]{1,0:T(8,128)S(1)}, u32[]{:S(2)}, u32[]{:S(2)}) collective-permute-start(f32[128,256]{1,0:T(8,128)S(1)} %get-tuple-element.41), channel_id=1, source_target_pairs={{0,1},{1,0},{2,3},{3,2},{4,5},{5,4},{6,7},{7,6},{8,9},{9,8},{10,11... | collective-permute-start | bytes 393224 | tf_op jit(solution)/shard_map/ppermute | solution.py:207
  17.4 2.0 %shard_map.74 = (f32[768,256]{1,0:T(8,128)S(1)}, f32[768,256]{1,0:T(8,128)S(1)}) custom-call(s32[16,32]{1,0:T(8,128)} %bitcast.12, bf16[768,768]{1,0:T(8,128)(2,1)S(1)} %get-tuple-element.35.high, bf16[768,768]{1,0:T(8,128)(2,1)S(1)} %get-tuple-element.36.low, bf16[768,256]{1,0:T(8,128)(2,1)S(1)} %get-tuple-element.37.m_high, ...), custom_call_target="tpu_custom_call" | custom-call | tf_op jit(solution)/shard_map/pallas_call | solution.py:193
  19.5 2.3 %collective-permute-done.2.below = f32[128,256]{1,0:T(8,128)S(1)} collective-permute-done((f32[128,256]{1,0:T(8,128)S(1)}, f32[128,256]{1,0:T(8,128)S(1)}, u32[]{:S(2)}, u32[]{:S(2)}) %collective-permute-start.2) | collective-permute-done | bytes 131104 | tf_op jit(solution)/shard_map/ppermute | solution.py:207
  22.2 11.4 %all_to_all.30.everything = f32[32,1,256]{2,1,0:T(1,128)S(1)} all-to-all(f32[32,1,256]{2,1,0:T(1,128)S(1)} %get-tuple-element.42), channel_id=1, replica_groups=mesh['z'=16,'c'=2,'y'=4,'x'=4] {'c','y','x'}, dimensions={0} | all-to-all | bytes 65536 | tf_op jit(solution)/shard_map/all_to_all | solution.py:211
  33.7 27.2 %all_to_all.31.everything = f32[16,1,256]{2,1,0:T(1,128)S(1)} all-to-all(f32[16,1,256]{2,1,0:T(1,128)S(1)} %shard_map.76), channel_id=1, replica_groups=mesh['z'=16,'c'=2,'y'=4,'x'=4] {'z'}, dimensions={0} | all-to-all | bytes 32768 | tf_op jit(solution)/shard_map/all_to_all | solution.py:211
  61.5 3.9 %collective-permute-start.5 = (f32[128,256]{1,0:T(8,128)S(1)}, f32[128,256]{1,0:T(8,128)S(1)}, u32[]{:S(2)}, u32[]{:S(2)}) collective-permute-start(f32[128,256]{1,0:T(8,128)S(1)} %get-tuple-element.51), channel_id=1, source_target_pairs={{0,16},{16,0},{32,48},{48,32},{64,80},{80,64},{96,112},{112,96},{1... | collective-permute-start | bytes 393224 | tf_op jit(solution)/shard_map/ppermute | solution.py:207
  65.4 2.2 %collective-permute-start.4 = (f32[128,256]{1,0:T(8,128)S(1)}, f32[128,256]{1,0:T(8,128)S(1)}, u32[]{:S(2)}, u32[]{:S(2)}) collective-permute-start(f32[128,256]{1,0:T(8,128)S(1)} %get-tuple-element.51), channel_id=1, source_target_pairs={{16,32},{32,16},{48,64},{64,48},{80,96},{96,80},{112,128},{128,112... | collective-permute-start | bytes 393224 | tf_op jit(solution)/shard_map/ppermute | solution.py:207
  68.3 3.8 %collective-permute-start.6 = (f32[128,256]{1,0:T(8,128)S(1)}, f32[128,256]{1,0:T(8,128)S(1)}, u32[]{:S(2)}, u32[]{:S(2)}) collective-permute-start(f32[128,256]{1,0:T(8,128)S(1)} %get-tuple-element.52), channel_id=1, source_target_pairs={{0,1},{1,0},{2,3},{3,2},{4,5},{5,4},{6,7},{7,6},{8,9},{9,8},{10,11... | collective-permute-start | bytes 393224 | tf_op jit(solution)/shard_map/ppermute | solution.py:207
  72.1 1.1 shard_map.78.local
  73.3 1.5 %collective-permute-done.6.below = f32[128,256]{1,0:T(8,128)S(1)} collective-permute-done((f32[128,256]{1,0:T(8,128)S(1)}, f32[128,256]{1,0:T(8,128)S(1)}, u32[]{:S(2)}, u32[]{:S(2)}) %collective-permute-start.6) | collective-permute-done | bytes 131104 | tf_op jit(solution)/shard_map/ppermute | solution.py:207
  75.2 13.9 %all_to_all.32.everything = f32[32,1,256]{2,1,0:T(1,128)S(1)} all-to-all(f32[32,1,256]{2,1,0:T(1,128)S(1)} %get-tuple-element.53), channel_id=1, replica_groups=mesh['z'=16,'c'=2,'y'=4,'x'=4] {'c','y','x'}, dimensions={0} | all-to-all | bytes 65536 | tf_op jit(solution)/shard_map/all_to_all | solution.py:211
  89.1 16.3 %all_to_all.33.everything = f32[16,1,256]{2,1,0:T(1,128)S(1)} all-to-all(f32[16,1,256]{2,1,0:T(1,128)S(1)} %shard_map.80), channel_id=1, replica_groups=mesh['z'=16,'c'=2,'y'=4,'x'=4] {'z'}, dimensions={0} | all-to-all | bytes 32768 | tf_op jit(solution)/shard_map/all_to_all | solution.py:211
  106.0 3.9 %collective-permute-start.9 = (f32[128,256]{1,0:T(8,128)S(1)}, f32[128,256]{1,0:T(8,128)S(1)}, u32[]{:S(2)}, u32[]{:S(2)}) collective-permute-start(f32[128,256]{1,0:T(8,128)S(1)} %get-tuple-element.58), channel_id=1, source_target_pairs={{0,16},{16,0},{32,48},{48,32},{64,80},{80,64},{96,112},{112,96},{1... | collective-permute-start | bytes 393224 | tf_op jit(solution)/shard_map/ppermute | solution.py:207
  110.0 2.2 %collective-permute-start.8 = (f32[128,256]{1,0:T(8,128)S(1)}, f32[128,256]{1,0:T(8,128)S(1)}, u32[]{:S(2)}, u32[]{:S(2)}) collective-permute-start(f32[128,256]{1,0:T(8,128)S(1)} %get-tuple-element.58), channel_id=1, source_target_pairs={{16,32},{32,16},{48,64},{64,48},{80,96},{96,80},{112,128},{128,112... | collective-permute-start | bytes 393224 | tf_op jit(solution)/shard_map/ppermute | solution.py:207
  112.2 0.7 collective-permute-start.11
  112.9 3.8 %collective-permute-start.10 = (f32[128,256]{1,0:T(8,128)S(1)}, f32[128,256]{1,0:T(8,128)S(1)}, u32[]{:S(2)}, u32[]{:S(2)}) collective-permute-start(f32[128,256]{1,0:T(8,128)S(1)} %get-tuple-element.59), channel_id=1, source_target_pairs={{0,1},{1,0},{2,3},{3,2},{4,5},{5,4},{6,7},{7,6},{8,9},{9,8},{10,11... | collective-permute-start | bytes 393224 | tf_op jit(solution)/shard_map/ppermute | solution.py:207
  116.7 1.1 shard_map.82.local
  117.8 1.6 %collective-permute-done.10.below = f32[128,256]{1,0:T(8,128)S(1)} collective-permute-done((f32[128,256]{1,0:T(8,128)S(1)}, f32[128,256]{1,0:T(8,128)S(1)}, u32[]{:S(2)}, u32[]{:S(2)}) %collective-permute-start.10) | collective-permute-done | bytes 131104 | tf_op jit(solution)/shard_map/ppermute | solution.py:207
  119.7 13.9 %all_to_all.34.everything = f32[32,1,256]{2,1,0:T(1,128)S(1)} all-to-all(f32[32,1,256]{2,1,0:T(1,128)S(1)} %get-tuple-element.60), channel_id=1, replica_groups=mesh['z'=16,'c'=2,'y'=4,'x'=4] {'c','y','x'}, dimensions={0} | all-to-all | bytes 65536 | tf_op jit(solution)/shard_map/all_to_all | solution.py:211
  133.6 16.3 %all_to_all.35.everything = f32[16,1,256]{2,1,0:T(1,128)S(1)} all-to-all(f32[16,1,256]{2,1,0:T(1,128)S(1)} %shard_map.84), channel_id=1, replica_groups=mesh['z'=16,'c'=2,'y'=4,'x'=4] {'z'}, dimensions={0} | all-to-all | bytes 32768 | tf_op jit(solution)/shard_map/all_to_all | solution.py:211
  149.9 1.1 shard_map.85
  (21 shorter events, 4.0 us)
Async XLA Ops:
  0.0 17.4 %copy-start = (f32[1,1,256,768]{3,2,1,0:T(8,128)S(1)}, f32[1,1,256,768]{3,2,1,0:T(8,128)}, u32[]{:S(2)}) copy-start(f32[1,1,256,768]{3,2,1,0:T(8,128)} %param.8) | copy-start | bytes 2359300
  4.1 15.4 %collective-permute-start.1 = (f32[128,256]{1,0:T(8,128)S(1)}, f32[128,256]{1,0:T(8,128)S(1)}, u32[]{:S(2)}, u32[]{:S(2)}) collective-permute-start(f32[128,256]{1,0:T(8,128)S(1)} %get-tuple-element.40), channel_id=1, source_target_pairs={{0,16},{16,0},{32,48},{48,32},{64,80},{80,64},{96,112},{112,96},{1... | collective-permute-start | bytes 393224 | tf_op jit(solution)/shard_map/ppermute | solution.py:207
  12.8 6.6 %collective-permute-start = (f32[128,256]{1,0:T(8,128)S(1)}, f32[128,256]{1,0:T(8,128)S(1)}, u32[]{:S(2)}, u32[]{:S(2)}) collective-permute-start(f32[128,256]{1,0:T(8,128)S(1)} %get-tuple-element.40), channel_id=1, source_target_pairs={{16,32},{32,16},{48,64},{64,48},{80,96},{96,80},{112,128},{128,112... | collective-permute-start | bytes 393224 | tf_op jit(solution)/shard_map/ppermute | solution.py:207
  14.8 4.7 %collective-permute-start.3 = (f32[128,256]{1,0:T(8,128)S(1)}, f32[128,256]{1,0:T(8,128)S(1)}, u32[]{:S(2)}, u32[]{:S(2)}) collective-permute-start(f32[128,256]{1,0:T(8,128)S(1)} %get-tuple-element.41), channel_id=1, source_target_pairs={{1,2},{2,1},{3,4},{4,3},{5,6},{6,5},{7,8},{8,7},{9,10},{10,9},{11,... | collective-permute-start | bytes 393224 | tf_op jit(solution)/shard_map/ppermute | solution.py:207
  15.4 6.3 %collective-permute-start.2 = (f32[128,256]{1,0:T(8,128)S(1)}, f32[128,256]{1,0:T(8,128)S(1)}, u32[]{:S(2)}, u32[]{:S(2)}) collective-permute-start(f32[128,256]{1,0:T(8,128)S(1)} %get-tuple-element.41), channel_id=1, source_target_pairs={{0,1},{1,0},{2,3},{3,2},{4,5},{5,4},{6,7},{7,6},{8,9},{9,8},{10,11... | collective-permute-start | bytes 393224 | tf_op jit(solution)/shard_map/ppermute | solution.py:207
  61.5 11.7 %collective-permute-start.5 = (f32[128,256]{1,0:T(8,128)S(1)}, f32[128,256]{1,0:T(8,128)S(1)}, u32[]{:S(2)}, u32[]{:S(2)}) collective-permute-start(f32[128,256]{1,0:T(8,128)S(1)} %get-tuple-element.51), channel_id=1, source_target_pairs={{0,16},{16,0},{32,48},{48,32},{64,80},{80,64},{96,112},{112,96},{1... | collective-permute-start | bytes 393224 | tf_op jit(solution)/shard_map/ppermute | solution.py:207
  65.4 7.8 %collective-permute-start.4 = (f32[128,256]{1,0:T(8,128)S(1)}, f32[128,256]{1,0:T(8,128)S(1)}, u32[]{:S(2)}, u32[]{:S(2)}) collective-permute-start(f32[128,256]{1,0:T(8,128)S(1)} %get-tuple-element.51), channel_id=1, source_target_pairs={{16,32},{32,16},{48,64},{64,48},{80,96},{96,80},{112,128},{128,112... | collective-permute-start | bytes 393224 | tf_op jit(solution)/shard_map/ppermute | solution.py:207
  67.7 5.6 %collective-permute-start.7 = (f32[128,256]{1,0:T(8,128)S(1)}, f32[128,256]{1,0:T(8,128)S(1)}, u32[]{:S(2)}, u32[]{:S(2)}) collective-permute-start(f32[128,256]{1,0:T(8,128)S(1)} %get-tuple-element.52), channel_id=1, source_target_pairs={{1,2},{2,1},{3,4},{4,3},{5,6},{6,5},{7,8},{8,7},{9,10},{10,9},{11,... | collective-permute-start | bytes 393224 | tf_op jit(solution)/shard_map/ppermute | solution.py:207
  68.3 6.5 %collective-permute-start.6 = (f32[128,256]{1,0:T(8,128)S(1)}, f32[128,256]{1,0:T(8,128)S(1)}, u32[]{:S(2)}, u32[]{:S(2)}) collective-permute-start(f32[128,256]{1,0:T(8,128)S(1)} %get-tuple-element.52), channel_id=1, source_target_pairs={{0,1},{1,0},{2,3},{3,2},{4,5},{5,4},{6,7},{7,6},{8,9},{9,8},{10,11... | collective-permute-start | bytes 393224 | tf_op jit(solution)/shard_map/ppermute | solution.py:207
  106.0 11.7 %collective-permute-start.9 = (f32[128,256]{1,0:T(8,128)S(1)}, f32[128,256]{1,0:T(8,128)S(1)}, u32[]{:S(2)}, u32[]{:S(2)}) collective-permute-start(f32[128,256]{1,0:T(8,128)S(1)} %get-tuple-element.58), channel_id=1, source_target_pairs={{0,16},{16,0},{32,48},{48,32},{64,80},{80,64},{96,112},{112,96},{1... | collective-permute-start | bytes 393224 | tf_op jit(solution)/shard_map/ppermute | solution.py:207
  110.0 7.8 %collective-permute-start.8 = (f32[128,256]{1,0:T(8,128)S(1)}, f32[128,256]{1,0:T(8,128)S(1)}, u32[]{:S(2)}, u32[]{:S(2)}) collective-permute-start(f32[128,256]{1,0:T(8,128)S(1)} %get-tuple-element.58), channel_id=1, source_target_pairs={{16,32},{32,16},{48,64},{64,48},{80,96},{96,80},{112,128},{128,112... | collective-permute-start | bytes 393224 | tf_op jit(solution)/shard_map/ppermute | solution.py:207
  112.2 5.6 %collective-permute-start.11 = (f32[128,256]{1,0:T(8,128)S(1)}, f32[128,256]{1,0:T(8,128)S(1)}, u32[]{:S(2)}, u32[]{:S(2)}) collective-permute-start(f32[128,256]{1,0:T(8,128)S(1)} %get-tuple-element.59), channel_id=1, source_target_pairs={{1,2},{2,1},{3,4},{4,3},{5,6},{6,5},{7,8},{8,7},{9,10},{10,9},{11,... | collective-permute-start | bytes 393224 | tf_op jit(solution)/shard_map/ppermute | solution.py:207
  112.9 6.5 %collective-permute-start.10 = (f32[128,256]{1,0:T(8,128)S(1)}, f32[128,256]{1,0:T(8,128)S(1)}, u32[]{:S(2)}, u32[]{:S(2)}) collective-permute-start(f32[128,256]{1,0:T(8,128)S(1)} %get-tuple-element.59), channel_id=1, source_target_pairs={{0,1},{1,0},{2,3},{3,2},{4,5},{5,4},{6,7},{7,6},{8,9},{9,8},{10,11... | collective-permute-start | bytes 393224 | tf_op jit(solution)/shard_map/ppermute | solution.py:207

commit v4 on v3

--- a/solution.py
+++ b/solution.py
@@ -47,28 +47,29 @@
 
 
 def chunk_copies(source, target, sems):
-    copies = [
+    return [
         pltpu.make_async_copy(source.at[:, pl.ds(number * COLS, COLS)], target.at[:, pl.ds(number * COLS, COLS)], sems.at[number])
         for number in range(CHUNKS)
     ]
-    for copy in copies:
-        copy.start()
-    return copies
-
-
-def first_kernel(orders, operator, warm, face_x, face_y, contact,
-                 high_out, low_out, faces_high_out, faces_low_out, slots_out, floor_out, m_out, m_high_out, m_low_out, near_x_out, near_y_out,
-                 orders_here, rows_here, warm_here, contact_here, sems, small_sems):
+
+
+def first_kernel(orders, operator, warm, loads, face_x, face_y, contact,
+                 high_out, low_out, faces_high_out, faces_low_out, slots_out, floor_out, rhs_out, m_out, m_high_out, m_low_out, near_x_out, near_y_out,
+                 orders_here, rows_here, warm_here, loads_here, contact_here, sems, small_sems):
     small = [
         pltpu.make_async_copy(face_x, slots_out.at[0:1, :], small_sems.at[0]),
         pltpu.make_async_copy(face_y, slots_out.at[1:2, :], small_sems.at[1]),
         pltpu.make_async_copy(orders, orders_here, small_sems.at[2]),
         pltpu.make_async_copy(warm, warm_here, small_sems.at[3]),
         pltpu.make_async_copy(contact, contact_here, small_sems.at[4]),
+        pltpu.make_async_copy(loads, loads_here, small_sems.at[5]),
     ]
-    for copy in small:
+    for copy in small[:5]:
         copy.start()
     copies = chunk_copies(operator, rows_here, sems)
+    for copy in copies:
+        copy.start()
+    small[5].start()
     small[0].wait()
     small[1].wait()
     column = jnp.concatenate([jnp.broadcast_to(slots_out[n : n + 1, :].astype(f32), (FSLOT, FSLOT)).T for n in range(2)], axis=0)
@@ -89,6 +90,9 @@
     near = jnp.zeros((2 * FSLOT, COLS), f32)
     for number, copy in enumerate(copies):
         copy.wait()
+        if number == 1:
+            small[5].wait()
+            rhs_out[...] = jnp.where(live_rows(order, COLS), loads_here[...].T, 0.0)
         part = chunk(number)
         high, low = split(jnp.where(live_rows(order, COLS), rows_here[:, part], 0.0))
         high_out[:, part] = high
@@ -104,16 +108,6 @@
 
 def order_of(orders):
     return orders[lax.axis_index(GY), lax.axis_index(GX)]
-
-
-def first_main_kernel(orders, high, low, m_high, m_low, loads, local_out, rhs_out, orders_here, orders_sem):
-    copy = pltpu.make_async_copy(orders, orders_here, orders_sem)
-    copy.start()
-    total = product(high[...], low[...], m_high[...], m_low[...])
-    copy.wait()
-    rhs = jnp.where(live_rows(order_of(orders_here), COLS), loads[...].T, 0.0)
-    rhs_out[...] = rhs
-    local_out[...] = total - rhs
 
 
 def main_kernel(high, low, m_high, m_low, rhs, local_out):
@@ -207,6 +201,16 @@
     return lax.ppermute(block, axis, route)
 
 
+def swapped_by_core(block, first):
+    route = []
+    rows = lax.axis_size(GY)
+    for core in range(lax.axis_size("c")):
+        for i in range((first + core) % 2, rows - 1, 2):
+            here = core * rows + i
+            route += [(here, here + 1), (here + 1, here)]
+    return lax.ppermute(block, NEAR, route)
+
+
 def from_everyone(copies, axis):
     return lax.all_to_all(copies, axis, split_axis=0, concat_axis=0, tiled=True)
 
@@ -223,25 +227,19 @@
     orders_here = pltpu.SMEM(orders.shape, jnp.int32)
     loads_here = pltpu.VMEM((COLS, ORDER), f32)
     sems = pltpu.SemaphoreType.DMA((CHUNKS,))
-    high, low, faces_high, faces_low, slots, floor, m, m_high, m_low, near_x, near_y = call(
+    high, low, faces_high, faces_low, slots, floor, rhs, m, m_high, m_low, near_x, near_y = call(
         first_kernel,
-        [square, square, faces, faces, keep((2, FSLOT), jnp.int32), keep((ORDER, FSLOT), bf16), state, half, half, face, face],
-        [far(x) for x in (orders, operator[0, 0], warm[0, 0], face_x[0], face_y[0], contact[0])],
-        [orders_here, rows_here, loads_here, pltpu.VMEM((1, ORDER), jnp.int32), sems, pltpu.SemaphoreType.DMA((5,))],
+        [square, square, faces, faces, keep((2, FSLOT), jnp.int32), keep((ORDER, FSLOT), bf16), state, state, half, half, face, face],
+        [far(x) for x in (orders, operator[0, 0], warm[0, 0], loads[0, 0], face_x[0], face_y[0], contact[0])],
+        [orders_here, rows_here, loads_here, loads_here, pltpu.VMEM((1, ORDER), jnp.int32), sems, pltpu.SemaphoreType.DMA((6,))],
     )
     for iteration in range(ITERS):
-        below = swapped(near_y, GY, 0)
-        above = swapped(near_y, GY, 1)
+        below = swapped_by_core(near_y, 0)
+        above = swapped_by_core(near_y, 1)
         outer = swapped(near_x, GX, 1)
         inner = swapped(near_x, GX, 0)
         matrices = [kept(x) for x in (high, low, m_high, m_low)]
-        if iteration == 0:
-            local, rhs = call(
-                first_main_kernel, [state, state], [far(orders), *matrices, kept(loads[0, 0])],
-                [orders_here, pltpu.SemaphoreType.DMA],
-            )
-        else:
-            (local,) = call(main_kernel, [state], [*matrices, kept(rhs)])
+        (local,) = call(main_kernel, [state], [*matrices, kept(rhs)])
         gradient, squares = call(
             gradient_kernel, [state, keep((lax.axis_size(NEAR), 1, COLS), f32)],
             [kept(x) for x in (slots, local, outer, inner, below, above)],

time: 152 us -> 151 us (level)
  waiting for transfers between devices: 5.44 us -> 10.3 us
  starting transfers between devices: 34.5 us -> 31.3 us
    ppermute x12 -> x6, starting transfers between devices: 34.5 us -> 23 us  [swapped(): return lax.ppermute(block, axis, route)]
    ppermute x0 -> x6, waiting for transfers between devices: none -> 9.19 us  [swapped_by_core(): return lax.ppermute(block, NEAR, route)]
    ppermute x0 -> x6, starting transfers between devices: none -> 8.31 us  [swapped_by_core(): return lax.ppermute(block, NEAR, route)]
    ppermute x12 -> x6, waiting for transfers between devices: 5.44 us -> 1.09 us  [swapped(): return lax.ppermute(block, axis, route)]
  transfers between devices with their start and end apart: 12 -> 12, of which waited for: 3 -> 6; matrix products, arithmetic and copies ran while one was open for 0% -> 0% of each run, Pallas kernels for 3% -> 2%
where the time goes in v4:
time: 151 us; the launch traced here: 150 us
  blocking collectives  97.9 us (65%)
  starting transfers between devices  31.3 us (21%)
  Pallas kernels  10.7 us (7%)
  waiting for transfers between devices  10.3 us (7%)
    all_to_all x6, blocking collectives, from_everyone(): return lax.all_to_all(copies, axis, split_axis=0, concat_axis=0, tiled=True)  97.9 us
    ppermute x6, starting transfers between devices, swapped(): return lax.ppermute(block, axis, route)  23 us
    pallas_call x13, Pallas kernels, call(): pl.pallas_call(kernel, out_shape=tuple((shape for shape, _ in outs)), in_...  10.7 us
    ppermute x6, waiting for transfers between devices, swapped_by_core(): return lax.ppermute(block, NEAR, route)  9.19 us
    ppermute x6, starting transfers between devices, swapped_by_core(): return lax.ppermute(block, NEAR, route)  8.31 us
  transfers between devices with their start and end apart: 12, of which 6 were waited for; matrix products, arithmetic and copies ran while one was open for 0% of the time, Pallas kernels for 2%

profile of v4, /device:TPU:1, one launch (start us, length us, event | category | flops | bytes accessed | tf_op | source)
XLA Modules:
  0.0 150.5 jit_solution(10269295447058698270)
XLA Ops:
  0.0 3.8 %shard_map.73 = (bf16[768,768]{1,0:T(8,128)(2,1)S(1)}, bf16[768,768]{1,0:T(8,128)(2,1)S(1)}, bf16[256,768]{1,0:T(8,128)(2,1)S(1)}, bf16[256,768]{1,0:T(8,128)(2,...) custom-call(s32[16,32]{1,0:T(8,128)} %bitcast.11, ...), custom_call_target="tpu_custom_call" | custom-call | tf_op jit(solution)/shard_map/pallas_call | solution.py:187
  3.8 8.7 %collective-permute-start.1 = (f32[128,256]{1,0:T(8,128)S(1)}, f32[128,256]{1,0:T(8,128)S(1)}, u32[]{:S(2)}, u32[]{:S(2)}) collective-permute-start(f32[128,256]{1,0:T(8,128)S(1)} %get-tuple-element.39), channel_id=1, source_target_pairs={{0,16},{16,0},{32,48},{48,32},{64,80},{80,64},{96,112},{112,96},{1... | collective-permute-start | bytes 393224 | tf_op jit(solution)/shard_map/ppermute | solution.py:201
  12.5 1.9 %collective-permute-start = (f32[128,256]{1,0:T(8,128)S(1)}, f32[128,256]{1,0:T(8,128)S(1)}, u32[]{:S(2)}, u32[]{:S(2)}) collective-permute-start(f32[128,256]{1,0:T(8,128)S(1)} %get-tuple-element.39), channel_id=1, source_target_pairs={{16,32},{32,16},{48,64},{64,48},{80,96},{96,80},{112,128},{128,112... | collective-permute-start | bytes 393224 | tf_op jit(solution)/shard_map/ppermute | solution.py:201
  14.4 1.9 %collective-permute-start.3 = (f32[128,256]{1,0:T(8,128)S(1)}, f32[128,256]{1,0:T(8,128)S(1)}, u32[]{:S(2)}, u32[]{:S(2)}) collective-permute-start(f32[128,256]{1,0:T(8,128)S(1)} %get-tuple-element.40), channel_id=1, source_target_pairs={{1,2},{2,1},{3,4},{4,3},{5,6},{6,5},{7,8},{8,7},{9,10},{10,9},{11,... | collective-permute-start | bytes 393224 | tf_op jit(solution)/shard_map/ppermute | solution.py:211
  17.1 1.1 shard_map.74.local
  18.2 0.9 collective-permute-done.outer
  19.1 2.6 %collective-permute-done.3.above = f32[128,256]{1,0:T(8,128)S(1)} collective-permute-done((f32[128,256]{1,0:T(8,128)S(1)}, f32[128,256]{1,0:T(8,128)S(1)}, u32[]{:S(2)}, u32[]{:S(2)}) %collective-permute-start.3) | collective-permute-done | bytes 131104 | tf_op jit(solution)/shard_map/ppermute | solution.py:211
  22.1 13.0 %all_to_all.30.everything = f32[32,1,256]{2,1,0:T(1,128)S(1)} all-to-all(f32[32,1,256]{2,1,0:T(1,128)S(1)} %get-tuple-element.41), channel_id=1, replica_groups=mesh['z'=16,'c'=2,'y'=4,'x'=4] {'c','y','x'}, dimensions={0} | all-to-all | bytes 65536 | tf_op jit(solution)/shard_map/all_to_all | solution.py:215
  35.1 25.2 %all_to_all.31.everything = f32[16,1,256]{2,1,0:T(1,128)S(1)} all-to-all(f32[16,1,256]{2,1,0:T(1,128)S(1)} %shard_map.76), channel_id=1, replica_groups=mesh['z'=16,'c'=2,'y'=4,'x'=4] {'z'}, dimensions={0} | all-to-all | bytes 32768 | tf_op jit(solution)/shard_map/all_to_all | solution.py:215
  61.0 3.9 %collective-permute-start.5 = (f32[128,256]{1,0:T(8,128)S(1)}, f32[128,256]{1,0:T(8,128)S(1)}, u32[]{:S(2)}, u32[]{:S(2)}) collective-permute-start(f32[128,256]{1,0:T(8,128)S(1)} %get-tuple-element.49), channel_id=1, source_target_pairs={{0,16},{16,0},{32,48},{48,32},{64,80},{80,64},{96,112},{112,96},{1... | collective-permute-start | bytes 393224 | tf_op jit(solution)/shard_map/ppermute | solution.py:201
  64.9 2.2 %collective-permute-start.4 = (f32[128,256]{1,0:T(8,128)S(1)}, f32[128,256]{1,0:T(8,128)S(1)}, u32[]{:S(2)}, u32[]{:S(2)}) collective-permute-start(f32[128,256]{1,0:T(8,128)S(1)} %get-tuple-element.49), channel_id=1, source_target_pairs={{16,32},{32,16},{48,64},{64,48},{80,96},{96,80},{112,128},{128,112... | collective-permute-start | bytes 393224 | tf_op jit(solution)/shard_map/ppermute | solution.py:201
  67.1 2.2 %collective-permute-start.7 = (f32[128,256]{1,0:T(8,128)S(1)}, f32[128,256]{1,0:T(8,128)S(1)}, u32[]{:S(2)}, u32[]{:S(2)}) collective-permute-start(f32[128,256]{1,0:T(8,128)S(1)} %get-tuple-element.50), channel_id=1, source_target_pairs={{1,2},{2,1},{3,4},{4,3},{5,6},{6,5},{7,8},{8,7},{9,10},{10,9},{11,... | collective-permute-start | bytes 393224 | tf_op jit(solution)/shard_map/ppermute | solution.py:211
  70.0 1.1 shard_map.78.local
  71.2 3.3 %collective-permute-done.7.above = f32[128,256]{1,0:T(8,128)S(1)} collective-permute-done((f32[128,256]{1,0:T(8,128)S(1)}, f32[128,256]{1,0:T(8,128)S(1)}, u32[]{:S(2)}, u32[]{:S(2)}) %collective-permute-start.7) | collective-permute-done | bytes 131104 | tf_op jit(solution)/shard_map/ppermute | solution.py:211
  74.9 12.8 %all_to_all.32.everything = f32[32,1,256]{2,1,0:T(1,128)S(1)} all-to-all(f32[32,1,256]{2,1,0:T(1,128)S(1)} %get-tuple-element.51), channel_id=1, replica_groups=mesh['z'=16,'c'=2,'y'=4,'x'=4] {'c','y','x'}, dimensions={0} | all-to-all | bytes 65536 | tf_op jit(solution)/shard_map/all_to_all | solution.py:215
  87.7 17.1 %all_to_all.33.everything = f32[16,1,256]{2,1,0:T(1,128)S(1)} all-to-all(f32[16,1,256]{2,1,0:T(1,128)S(1)} %shard_map.80), channel_id=1, replica_groups=mesh['z'=16,'c'=2,'y'=4,'x'=4] {'z'}, dimensions={0} | all-to-all | bytes 32768 | tf_op jit(solution)/shard_map/all_to_all | solution.py:215
  105.5 3.9 %collective-permute-start.9 = (f32[128,256]{1,0:T(8,128)S(1)}, f32[128,256]{1,0:T(8,128)S(1)}, u32[]{:S(2)}, u32[]{:S(2)}) collective-permute-start(f32[128,256]{1,0:T(8,128)S(1)} %get-tuple-element.56), channel_id=1, source_target_pairs={{0,16},{16,0},{32,48},{48,32},{64,80},{80,64},{96,112},{112,96},{1... | collective-permute-start | bytes 393224 | tf_op jit(solution)/shard_map/ppermute | solution.py:201
  109.5 2.2 %collective-permute-start.8 = (f32[128,256]{1,0:T(8,128)S(1)}, f32[128,256]{1,0:T(8,128)S(1)}, u32[]{:S(2)}, u32[]{:S(2)}) collective-permute-start(f32[128,256]{1,0:T(8,128)S(1)} %get-tuple-element.56), channel_id=1, source_target_pairs={{16,32},{32,16},{48,64},{64,48},{80,96},{96,80},{112,128},{128,112... | collective-permute-start | bytes 393224 | tf_op jit(solution)/shard_map/ppermute | solution.py:201
  111.7 2.2 %collective-permute-start.11 = (f32[128,256]{1,0:T(8,128)S(1)}, f32[128,256]{1,0:T(8,128)S(1)}, u32[]{:S(2)}, u32[]{:S(2)}) collective-permute-start(f32[128,256]{1,0:T(8,128)S(1)} %get-tuple-element.57), channel_id=1, source_target_pairs={{1,2},{2,1},{3,4},{4,3},{5,6},{6,5},{7,8},{8,7},{9,10},{10,9},{11,... | collective-permute-start | bytes 393224 | tf_op jit(solution)/shard_map/ppermute | solution.py:211
  114.6 1.1 shard_map.82.local
  115.7 3.3 %collective-permute-done.11.above = f32[128,256]{1,0:T(8,128)S(1)} collective-permute-done((f32[128,256]{1,0:T(8,128)S(1)}, f32[128,256]{1,0:T(8,128)S(1)}, u32[]{:S(2)}, u32[]{:S(2)}) %collective-permute-start.11) | collective-permute-done | bytes 131104 | tf_op jit(solution)/shard_map/ppermute | solution.py:211
  119.5 12.8 %all_to_all.34.everything = f32[32,1,256]{2,1,0:T(1,128)S(1)} all-to-all(f32[32,1,256]{2,1,0:T(1,128)S(1)} %get-tuple-element.58), channel_id=1, replica_groups=mesh['z'=16,'c'=2,'y'=4,'x'=4] {'c','y','x'}, dimensions={0} | all-to-all | bytes 65536 | tf_op jit(solution)/shard_map/all_to_all | solution.py:215
  132.3 17.1 %all_to_all.35.everything = f32[16,1,256]{2,1,0:T(1,128)S(1)} all-to-all(f32[16,1,256]{2,1,0:T(1,128)S(1)} %shard_map.84), channel_id=1, replica_groups=mesh['z'=16,'c'=2,'y'=4,'x'=4] {'z'}, dimensions={0} | all-to-all | bytes 32768 | tf_op jit(solution)/shard_map/all_to_all | solution.py:215
  149.4 1.1 shard_map.85
  (19 shorter events, 4.8 us)
Async XLA Ops:
  3.8 14.4 %collective-permute-start.1 = (f32[128,256]{1,0:T(8,128)S(1)}, f32[128,256]{1,0:T(8,128)S(1)}, u32[]{:S(2)}, u32[]{:S(2)}) collective-permute-start(f32[128,256]{1,0:T(8,128)S(1)} %get-tuple-element.39), channel_id=1, source_target_pairs={{0,16},{16,0},{32,48},{48,32},{64,80},{80,64},{96,112},{112,96},{1... | collective-permute-start | bytes 393224 | tf_op jit(solution)/shard_map/ppermute | solution.py:201
  12.5 6.6 %collective-permute-start = (f32[128,256]{1,0:T(8,128)S(1)}, f32[128,256]{1,0:T(8,128)S(1)}, u32[]{:S(2)}, u32[]{:S(2)}) collective-permute-start(f32[128,256]{1,0:T(8,128)S(1)} %get-tuple-element.39), channel_id=1, source_target_pairs={{16,32},{32,16},{48,64},{64,48},{80,96},{96,80},{112,128},{128,112... | collective-permute-start | bytes 393224 | tf_op jit(solution)/shard_map/ppermute | solution.py:201
  14.4 7.2 %collective-permute-start.3 = (f32[128,256]{1,0:T(8,128)S(1)}, f32[128,256]{1,0:T(8,128)S(1)}, u32[]{:S(2)}, u32[]{:S(2)}) collective-permute-start(f32[128,256]{1,0:T(8,128)S(1)} %get-tuple-element.40), channel_id=1, source_target_pairs={{1,2},{2,1},{3,4},{4,3},{5,6},{6,5},{7,8},{8,7},{9,10},{10,9},{11,... | collective-permute-start | bytes 393224 | tf_op jit(solution)/shard_map/ppermute | solution.py:211
  16.4 5.3 %collective-permute-start.2 = (f32[128,256]{1,0:T(8,128)S(1)}, f32[128,256]{1,0:T(8,128)S(1)}, u32[]{:S(2)}, u32[]{:S(2)}) collective-permute-start(f32[128,256]{1,0:T(8,128)S(1)} %get-tuple-element.40), channel_id=1, source_target_pairs={{0,1},{1,0},{2,3},{3,2},{4,5},{5,4},{6,7},{7,6},{8,9},{9,8},{10,11... | collective-permute-start | bytes 393224 | tf_op jit(solution)/shard_map/ppermute | solution.py:211
  61.0 10.2 %collective-permute-start.5 = (f32[128,256]{1,0:T(8,128)S(1)}, f32[128,256]{1,0:T(8,128)S(1)}, u32[]{:S(2)}, u32[]{:S(2)}) collective-permute-start(f32[128,256]{1,0:T(8,128)S(1)} %get-tuple-element.49), channel_id=1, source_target_pairs={{0,16},{16,0},{32,48},{48,32},{64,80},{80,64},{96,112},{112,96},{1... | collective-permute-start | bytes 393224 | tf_op jit(solution)/shard_map/ppermute | solution.py:201
  64.9 6.3 %collective-permute-start.4 = (f32[128,256]{1,0:T(8,128)S(1)}, f32[128,256]{1,0:T(8,128)S(1)}, u32[]{:S(2)}, u32[]{:S(2)}) collective-permute-start(f32[128,256]{1,0:T(8,128)S(1)} %get-tuple-element.49), channel_id=1, source_target_pairs={{16,32},{32,16},{48,64},{64,48},{80,96},{96,80},{112,128},{128,112... | collective-permute-start | bytes 393224 | tf_op jit(solution)/shard_map/ppermute | solution.py:201
  67.1 7.4 %collective-permute-start.7 = (f32[128,256]{1,0:T(8,128)S(1)}, f32[128,256]{1,0:T(8,128)S(1)}, u32[]{:S(2)}, u32[]{:S(2)}) collective-permute-start(f32[128,256]{1,0:T(8,128)S(1)} %get-tuple-element.50), channel_id=1, source_target_pairs={{1,2},{2,1},{3,4},{4,3},{5,6},{6,5},{7,8},{8,7},{9,10},{10,9},{11,... | collective-permute-start | bytes 393224 | tf_op jit(solution)/shard_map/ppermute | solution.py:211
  69.3 5.2 %collective-permute-start.6 = (f32[128,256]{1,0:T(8,128)S(1)}, f32[128,256]{1,0:T(8,128)S(1)}, u32[]{:S(2)}, u32[]{:S(2)}) collective-permute-start(f32[128,256]{1,0:T(8,128)S(1)} %get-tuple-element.50), channel_id=1, source_target_pairs={{0,1},{1,0},{2,3},{3,2},{4,5},{5,4},{6,7},{7,6},{8,9},{9,8},{10,11... | collective-permute-start | bytes 393224 | tf_op jit(solution)/shard_map/ppermute | solution.py:211
  105.5 10.2 %collective-permute-start.9 = (f32[128,256]{1,0:T(8,128)S(1)}, f32[128,256]{1,0:T(8,128)S(1)}, u32[]{:S(2)}, u32[]{:S(2)}) collective-permute-start(f32[128,256]{1,0:T(8,128)S(1)} %get-tuple-element.56), channel_id=1, source_target_pairs={{0,16},{16,0},{32,48},{48,32},{64,80},{80,64},{96,112},{112,96},{1... | collective-permute-start | bytes 393224 | tf_op jit(solution)/shard_map/ppermute | solution.py:201
  109.5 6.3 %collective-permute-start.8 = (f32[128,256]{1,0:T(8,128)S(1)}, f32[128,256]{1,0:T(8,128)S(1)}, u32[]{:S(2)}, u32[]{:S(2)}) collective-permute-start(f32[128,256]{1,0:T(8,128)S(1)} %get-tuple-element.56), channel_id=1, source_target_pairs={{16,32},{32,16},{48,64},{64,48},{80,96},{96,80},{112,128},{128,112... | collective-permute-start | bytes 393224 | tf_op jit(solution)/shard_map/ppermute | solution.py:201
  111.7 7.4 %collective-permute-start.11 = (f32[128,256]{1,0:T(8,128)S(1)}, f32[128,256]{1,0:T(8,128)S(1)}, u32[]{:S(2)}, u32[]{:S(2)}) collective-permute-start(f32[128,256]{1,0:T(8,128)S(1)} %get-tuple-element.57), channel_id=1, source_target_pairs={{1,2},{2,1},{3,4},{4,3},{5,6},{6,5},{7,8},{8,7},{9,10},{10,9},{11,... | collective-permute-start | bytes 393224 | tf_op jit(solution)/shard_map/ppermute | solution.py:211
  113.9 5.2 %collective-permute-start.10 = (f32[128,256]{1,0:T(8,128)S(1)}, f32[128,256]{1,0:T(8,128)S(1)}, u32[]{:S(2)}, u32[]{:S(2)}) collective-permute-start(f32[128,256]{1,0:T(8,128)S(1)} %get-tuple-element.57), channel_id=1, source_target_pairs={{0,1},{1,0},{2,3},{3,2},{4,5},{5,4},{6,7},{7,6},{8,9},{9,8},{10,11... | collective-permute-start | bytes 393224 | tf_op jit(solution)/shard_map/ppermute | solution.py:211

commit v5 on v4

--- a/solution.py
+++ b/solution.py
@@ -13,10 +13,10 @@
 COLS = 256
 ITERS = 3
 CHUNKS = ORDER // COLS
-GX = ("z", "c")
+GX = ("z1", "z0", "c")
 GY = ("y", "x")
 NEAR = ("c", "y", "x")
-FAR = ("z",)
+FAR = ("z0", "z1")
 
 step_length = 0.5
 epsilon = 1e-06
@@ -208,7 +208,7 @@
         for i in range((first + core) % 2, rows - 1, 2):
             here = core * rows + i
             route += [(here, here + 1), (here + 1, here)]
-    return lax.ppermute(block, NEAR, route)
+    return lax.ppermute(block, ("c", "y", "x"), route)
 
 
 def from_everyone(copies, axis):
@@ -264,7 +264,7 @@
 
 def solution(mesh):
     shape = dict(mesh.shape)
-    finer = Mesh(mesh.devices.reshape(shape["gx"] // 2, 2, 4, shape["gy"] // 4), ("z", "c", "y", "x"))
+    finer = Mesh(mesh.devices.reshape(4, shape["gx"] // 8, 2, 4, shape["gy"] // 4), ("z1", "z0", "c", "y", "x"))
     in_specs = (
         P(GX, GY, None, None),
         P(GX, GY, None, None),

time: 151 us -> 151 us (level)
  transfers between devices with their start and end apart: 12 -> 12, of which waited for: 6 -> 4; matrix products, arithmetic and copies ran while one was open for 0% -> 0% of each run, Pallas kernels for 2% -> 2%
where the time goes in v5:
time: 151 us; the launch traced here: 150 us
  blocking collectives  97.7 us (65%)
  starting transfers between devices  31.5 us (21%)
  Pallas kernels  10.7 us (7%)
  waiting for transfers between devices  10.1 us (7%)
    all_to_all x6, blocking collectives, from_everyone(): return lax.all_to_all(copies, axis, split_axis=0, concat_axis=0, tiled=True)  97.7 us
    ppermute x6, starting transfers between devices, swapped(): return lax.ppermute(block, axis, route)  23.2 us
    pallas_call x13, Pallas kernels, call(): pl.pallas_call(kernel, out_shape=tuple((shape for shape, _ in outs)), in_...  10.7 us
    ppermute x6, waiting for transfers between devices, swapped_by_core(): return lax.ppermute(block, ('c', 'y', 'x'), route)  9.18 us
    ppermute x6, starting transfers between devices, swapped_by_core(): return lax.ppermute(block, ('c', 'y', 'x'), route)  8.31 us
  transfers between devices with their start and end apart: 12, of which 4 were waited for; matrix products, arithmetic and copies ran while one was open for 0% of the time, Pallas kernels for 2%

profile of v5, /device:TPU:1, one launch (start us, length us, event | category | flops | bytes accessed | tf_op | source)
XLA Modules:
  0.0 150.3 jit_solution(16399319689390393124)
XLA Ops:
  0.0 3.8 %shard_map.73 = (bf16[768,768]{1,0:T(8,128)(2,1)S(1)}, bf16[768,768]{1,0:T(8,128)(2,1)S(1)}, bf16[256,768]{1,0:T(8,128)(2,1)S(1)}, bf16[256,768]{1,0:T(8,128)(2,...) custom-call(s32[16,32]{1,0:T(8,128)} %bitcast.11, ...), custom_call_target="tpu_custom_call" | custom-call | tf_op jit(solution)/shard_map/pallas_call | solution.py:187
  3.8 8.7 %collective-permute-start.1 = (f32[128,256]{1,0:T(8,128)S(1)}, f32[128,256]{1,0:T(8,128)S(1)}, u32[]{:S(2)}, u32[]{:S(2)}) collective-permute-start(f32[128,256]{1,0:T(8,128)S(1)} %get-tuple-element.39), channel_id=1, source_target_pairs={{0,16},{16,0},{32,48},{48,32},{64,80},{80,64},{96,112},{112,96},{1... | collective-permute-start | bytes 393224 | tf_op jit(solution)/shard_map/ppermute | solution.py:201
  12.5 1.9 %collective-permute-start = (f32[128,256]{1,0:T(8,128)S(1)}, f32[128,256]{1,0:T(8,128)S(1)}, u32[]{:S(2)}, u32[]{:S(2)}) collective-permute-start(f32[128,256]{1,0:T(8,128)S(1)} %get-tuple-element.39), channel_id=1, source_target_pairs={{16,32},{32,16},{48,64},{64,48},{80,96},{96,80},{112,128},{128,112... | collective-permute-start | bytes 393224 | tf_op jit(solution)/shard_map/ppermute | solution.py:201
  14.4 1.9 %collective-permute-start.3 = (f32[128,256]{1,0:T(8,128)S(1)}, f32[128,256]{1,0:T(8,128)S(1)}, u32[]{:S(2)}, u32[]{:S(2)}) collective-permute-start(f32[128,256]{1,0:T(8,128)S(1)} %get-tuple-element.40), channel_id=1, source_target_pairs={{1,2},{2,1},{3,4},{4,3},{5,6},{6,5},{7,8},{8,7},{9,10},{10,9},{11,... | collective-permute-start | bytes 393224 | tf_op jit(solution)/shard_map/ppermute | solution.py:211
  17.1 1.1 shard_map.74.local
  18.2 0.9 collective-permute-done.outer
  19.1 2.6 %collective-permute-done.3.above = f32[128,256]{1,0:T(8,128)S(1)} collective-permute-done((f32[128,256]{1,0:T(8,128)S(1)}, f32[128,256]{1,0:T(8,128)S(1)}, u32[]{:S(2)}, u32[]{:S(2)}) %collective-permute-start.3) | collective-permute-done | bytes 131104 | tf_op jit(solution)/shard_map/ppermute | solution.py:211
  22.1 13.0 %all_to_all.30.everything = f32[32,1,256]{2,1,0:T(1,128)S(1)} all-to-all(f32[32,1,256]{2,1,0:T(1,128)S(1)} %get-tuple-element.41), channel_id=1, replica_groups=mesh['z1'=4,'z0'=4,'c'=2,'y'=4,'x'=4] {'c','y','x'}, dimensions={0} | all-to-all | bytes 65536 | tf_op jit(solution)/shard_map/all_to_all | solution.py:215
  35.1 25.1 %all_to_all.31.everything = f32[16,1,256]{2,1,0:T(1,128)S(1)} all-to-all(f32[16,1,256]{2,1,0:T(1,128)S(1)} %shard_map.76), channel_id=1, replica_groups=mesh['z1'=4,'z0'=4,'c'=2,'y'=4,'x'=4] {'z0','z1'}, dimensions={0} | all-to-all | bytes 32768 | tf_op jit(solution)/shard_map/all_to_all | solution.py:215
  60.8 4.0 %collective-permute-start.5 = (f32[128,256]{1,0:T(8,128)S(1)}, f32[128,256]{1,0:T(8,128)S(1)}, u32[]{:S(2)}, u32[]{:S(2)}) collective-permute-start(f32[128,256]{1,0:T(8,128)S(1)} %get-tuple-element.49), channel_id=1, source_target_pairs={{0,16},{16,0},{32,48},{48,32},{64,80},{80,64},{96,112},{112,96},{1... | collective-permute-start | bytes 393224 | tf_op jit(solution)/shard_map/ppermute | solution.py:201
  64.8 2.3 %collective-permute-start.4 = (f32[128,256]{1,0:T(8,128)S(1)}, f32[128,256]{1,0:T(8,128)S(1)}, u32[]{:S(2)}, u32[]{:S(2)}) collective-permute-start(f32[128,256]{1,0:T(8,128)S(1)} %get-tuple-element.49), channel_id=1, source_target_pairs={{16,32},{32,16},{48,64},{64,48},{80,96},{96,80},{112,128},{128,112... | collective-permute-start | bytes 393224 | tf_op jit(solution)/shard_map/ppermute | solution.py:201
  67.1 2.2 %collective-permute-start.7 = (f32[128,256]{1,0:T(8,128)S(1)}, f32[128,256]{1,0:T(8,128)S(1)}, u32[]{:S(2)}, u32[]{:S(2)}) collective-permute-start(f32[128,256]{1,0:T(8,128)S(1)} %get-tuple-element.50), channel_id=1, source_target_pairs={{1,2},{2,1},{3,4},{4,3},{5,6},{6,5},{7,8},{8,7},{9,10},{10,9},{11,... | collective-permute-start | bytes 393224 | tf_op jit(solution)/shard_map/ppermute | solution.py:211
  70.0 1.1 shard_map.78.local
  71.1 3.3 %collective-permute-done.7.above = f32[128,256]{1,0:T(8,128)S(1)} collective-permute-done((f32[128,256]{1,0:T(8,128)S(1)}, f32[128,256]{1,0:T(8,128)S(1)}, u32[]{:S(2)}, u32[]{:S(2)}) %collective-permute-start.7) | collective-permute-done | bytes 131104 | tf_op jit(solution)/shard_map/ppermute | solution.py:211
  74.8 12.8 %all_to_all.32.everything = f32[32,1,256]{2,1,0:T(1,128)S(1)} all-to-all(f32[32,1,256]{2,1,0:T(1,128)S(1)} %get-tuple-element.51), channel_id=1, replica_groups=mesh['z1'=4,'z0'=4,'c'=2,'y'=4,'x'=4] {'c','y','x'}, dimensions={0} | all-to-all | bytes 65536 | tf_op jit(solution)/shard_map/all_to_all | solution.py:215
  87.7 17.1 %all_to_all.33.everything = f32[16,1,256]{2,1,0:T(1,128)S(1)} all-to-all(f32[16,1,256]{2,1,0:T(1,128)S(1)} %shard_map.80), channel_id=1, replica_groups=mesh['z1'=4,'z0'=4,'c'=2,'y'=4,'x'=4] {'z0','z1'}, dimensions={0} | all-to-all | bytes 32768 | tf_op jit(solution)/shard_map/all_to_all | solution.py:215
  105.4 4.0 %collective-permute-start.9 = (f32[128,256]{1,0:T(8,128)S(1)}, f32[128,256]{1,0:T(8,128)S(1)}, u32[]{:S(2)}, u32[]{:S(2)}) collective-permute-start(f32[128,256]{1,0:T(8,128)S(1)} %get-tuple-element.56), channel_id=1, source_target_pairs={{0,16},{16,0},{32,48},{48,32},{64,80},{80,64},{96,112},{112,96},{1... | collective-permute-start | bytes 393224 | tf_op jit(solution)/shard_map/ppermute | solution.py:201
  109.4 2.3 %collective-permute-start.8 = (f32[128,256]{1,0:T(8,128)S(1)}, f32[128,256]{1,0:T(8,128)S(1)}, u32[]{:S(2)}, u32[]{:S(2)}) collective-permute-start(f32[128,256]{1,0:T(8,128)S(1)} %get-tuple-element.56), channel_id=1, source_target_pairs={{16,32},{32,16},{48,64},{64,48},{80,96},{96,80},{112,128},{128,112... | collective-permute-start | bytes 393224 | tf_op jit(solution)/shard_map/ppermute | solution.py:201
  111.7 2.2 %collective-permute-start.11 = (f32[128,256]{1,0:T(8,128)S(1)}, f32[128,256]{1,0:T(8,128)S(1)}, u32[]{:S(2)}, u32[]{:S(2)}) collective-permute-start(f32[128,256]{1,0:T(8,128)S(1)} %get-tuple-element.57), channel_id=1, source_target_pairs={{1,2},{2,1},{3,4},{4,3},{5,6},{6,5},{7,8},{8,7},{9,10},{10,9},{11,... | collective-permute-start | bytes 393224 | tf_op jit(solution)/shard_map/ppermute | solution.py:211
  114.5 1.1 shard_map.82.local
  115.7 3.3 %collective-permute-done.11.above = f32[128,256]{1,0:T(8,128)S(1)} collective-permute-done((f32[128,256]{1,0:T(8,128)S(1)}, f32[128,256]{1,0:T(8,128)S(1)}, u32[]{:S(2)}, u32[]{:S(2)}) %collective-permute-start.11) | collective-permute-done | bytes 131104 | tf_op jit(solution)/shard_map/ppermute | solution.py:211
  119.4 12.8 %all_to_all.34.everything = f32[32,1,256]{2,1,0:T(1,128)S(1)} all-to-all(f32[32,1,256]{2,1,0:T(1,128)S(1)} %get-tuple-element.58), channel_id=1, replica_groups=mesh['z1'=4,'z0'=4,'c'=2,'y'=4,'x'=4] {'c','y','x'}, dimensions={0} | all-to-all | bytes 65536 | tf_op jit(solution)/shard_map/all_to_all | solution.py:215
  132.2 17.1 %all_to_all.35.everything = f32[16,1,256]{2,1,0:T(1,128)S(1)} all-to-all(f32[16,1,256]{2,1,0:T(1,128)S(1)} %shard_map.84), channel_id=1, replica_groups=mesh['z1'=4,'z0'=4,'c'=2,'y'=4,'x'=4] {'z0','z1'}, dimensions={0} | all-to-all | bytes 32768 | tf_op jit(solution)/shard_map/all_to_all | solution.py:215
  149.2 1.1 shard_map.85
  (19 shorter events, 4.7 us)
Async XLA Ops:
  3.8 14.4 %collective-permute-start.1 = (f32[128,256]{1,0:T(8,128)S(1)}, f32[128,256]{1,0:T(8,128)S(1)}, u32[]{:S(2)}, u32[]{:S(2)}) collective-permute-start(f32[128,256]{1,0:T(8,128)S(1)} %get-tuple-element.39), channel_id=1, source_target_pairs={{0,16},{16,0},{32,48},{48,32},{64,80},{80,64},{96,112},{112,96},{1... | collective-permute-start | bytes 393224 | tf_op jit(solution)/shard_map/ppermute | solution.py:201
  12.5 6.6 %collective-permute-start = (f32[128,256]{1,0:T(8,128)S(1)}, f32[128,256]{1,0:T(8,128)S(1)}, u32[]{:S(2)}, u32[]{:S(2)}) collective-permute-start(f32[128,256]{1,0:T(8,128)S(1)} %get-tuple-element.39), channel_id=1, source_target_pairs={{16,32},{32,16},{48,64},{64,48},{80,96},{96,80},{112,128},{128,112... | collective-permute-start | bytes 393224 | tf_op jit(solution)/shard_map/ppermute | solution.py:201
  14.4 7.2 %collective-permute-start.3 = (f32[128,256]{1,0:T(8,128)S(1)}, f32[128,256]{1,0:T(8,128)S(1)}, u32[]{:S(2)}, u32[]{:S(2)}) collective-permute-start(f32[128,256]{1,0:T(8,128)S(1)} %get-tuple-element.40), channel_id=1, source_target_pairs={{1,2},{2,1},{3,4},{4,3},{5,6},{6,5},{7,8},{8,7},{9,10},{10,9},{11,... | collective-permute-start | bytes 393224 | tf_op jit(solution)/shard_map/ppermute | solution.py:211
  16.4 5.3 %collective-permute-start.2 = (f32[128,256]{1,0:T(8,128)S(1)}, f32[128,256]{1,0:T(8,128)S(1)}, u32[]{:S(2)}, u32[]{:S(2)}) collective-permute-start(f32[128,256]{1,0:T(8,128)S(1)} %get-tuple-element.40), channel_id=1, source_target_pairs={{0,1},{1,0},{2,3},{3,2},{4,5},{5,4},{6,7},{7,6},{8,9},{9,8},{10,11... | collective-permute-start | bytes 393224 | tf_op jit(solution)/shard_map/ppermute | solution.py:211
  60.8 10.3 %collective-permute-start.5 = (f32[128,256]{1,0:T(8,128)S(1)}, f32[128,256]{1,0:T(8,128)S(1)}, u32[]{:S(2)}, u32[]{:S(2)}) collective-permute-start(f32[128,256]{1,0:T(8,128)S(1)} %get-tuple-element.49), channel_id=1, source_target_pairs={{0,16},{16,0},{32,48},{48,32},{64,80},{80,64},{96,112},{112,96},{1... | collective-permute-start | bytes 393224 | tf_op jit(solution)/shard_map/ppermute | solution.py:201
  64.8 6.3 %collective-permute-start.4 = (f32[128,256]{1,0:T(8,128)S(1)}, f32[128,256]{1,0:T(8,128)S(1)}, u32[]{:S(2)}, u32[]{:S(2)}) collective-permute-start(f32[128,256]{1,0:T(8,128)S(1)} %get-tuple-element.49), channel_id=1, source_target_pairs={{16,32},{32,16},{48,64},{64,48},{80,96},{96,80},{112,128},{128,112... | collective-permute-start | bytes 393224 | tf_op jit(solution)/shard_map/ppermute | solution.py:201
  67.1 7.3 %collective-permute-start.7 = (f32[128,256]{1,0:T(8,128)S(1)}, f32[128,256]{1,0:T(8,128)S(1)}, u32[]{:S(2)}, u32[]{:S(2)}) collective-permute-start(f32[128,256]{1,0:T(8,128)S(1)} %get-tuple-element.50), channel_id=1, source_target_pairs={{1,2},{2,1},{3,4},{4,3},{5,6},{6,5},{7,8},{8,7},{9,10},{10,9},{11,... | collective-permute-start | bytes 393224 | tf_op jit(solution)/shard_map/ppermute | solution.py:211
  69.3 5.1 %collective-permute-start.6 = (f32[128,256]{1,0:T(8,128)S(1)}, f32[128,256]{1,0:T(8,128)S(1)}, u32[]{:S(2)}, u32[]{:S(2)}) collective-permute-start(f32[128,256]{1,0:T(8,128)S(1)} %get-tuple-element.50), channel_id=1, source_target_pairs={{0,1},{1,0},{2,3},{3,2},{4,5},{5,4},{6,7},{7,6},{8,9},{9,8},{10,11... | collective-permute-start | bytes 393224 | tf_op jit(solution)/shard_map/ppermute | solution.py:211
  105.4 10.3 %collective-permute-start.9 = (f32[128,256]{1,0:T(8,128)S(1)}, f32[128,256]{1,0:T(8,128)S(1)}, u32[]{:S(2)}, u32[]{:S(2)}) collective-permute-start(f32[128,256]{1,0:T(8,128)S(1)} %get-tuple-element.56), channel_id=1, source_target_pairs={{0,16},{16,0},{32,48},{48,32},{64,80},{80,64},{96,112},{112,96},{1... | collective-permute-start | bytes 393224 | tf_op jit(solution)/shard_map/ppermute | solution.py:201
  109.4 6.3 %collective-permute-start.8 = (f32[128,256]{1,0:T(8,128)S(1)}, f32[128,256]{1,0:T(8,128)S(1)}, u32[]{:S(2)}, u32[]{:S(2)}) collective-permute-start(f32[128,256]{1,0:T(8,128)S(1)} %get-tuple-element.56), channel_id=1, source_target_pairs={{16,32},{32,16},{48,64},{64,48},{80,96},{96,80},{112,128},{128,112... | collective-permute-start | bytes 393224 | tf_op jit(solution)/shard_map/ppermute | solution.py:201
  111.7 7.3 %collective-permute-start.11 = (f32[128,256]{1,0:T(8,128)S(1)}, f32[128,256]{1,0:T(8,128)S(1)}, u32[]{:S(2)}, u32[]{:S(2)}) collective-permute-start(f32[128,256]{1,0:T(8,128)S(1)} %get-tuple-element.57), channel_id=1, source_target_pairs={{1,2},{2,1},{3,4},{4,3},{5,6},{6,5},{7,8},{8,7},{9,10},{10,9},{11,... | collective-permute-start | bytes 393224 | tf_op jit(solution)/shard_map/ppermute | solution.py:211
  113.9 5.1 %collective-permute-start.10 = (f32[128,256]{1,0:T(8,128)S(1)}, f32[128,256]{1,0:T(8,128)S(1)}, u32[]{:S(2)}, u32[]{:S(2)}) collective-permute-start(f32[128,256]{1,0:T(8,128)S(1)} %get-tuple-element.57), channel_id=1, source_target_pairs={{0,1},{1,0},{2,3},{3,2},{4,5},{5,4},{6,7},{7,6},{8,9},{9,8},{10,11... | collective-permute-start | bytes 393224 | tf_op jit(solution)/shard_map/ppermute | solution.py:211

commit v6 on v5

--- a/solution.py
+++ b/solution.py
@@ -130,20 +130,19 @@
     squares_out[...] = jnp.broadcast_to(squares[None], squares_out.shape)
 
 
-def updated(everything, m, gradient, floor, count):
+def update_kernel(count, everything, m, gradient, floor, faces_high, faces_low, m_out, m_high_out, m_low_out, near_x_out, near_y_out):
     squares = jnp.sum(everything[...], axis=0)
     rate = step_length / jnp.sqrt(squares / count + epsilon)
-    lowest = jnp.concatenate([floor[...].astype(f32)] * (COLS // FSLOT), axis=1)
-    return jnp.maximum(m[...] - gradient[...] * rate, lowest)
-
-
-def update_kernel(count, everything, m, gradient, floor, faces_high, faces_low, m_out, m_high_out, m_low_out, near_x_out, near_y_out):
-    new = updated(everything, m, gradient, floor, count)
-    m_out[...] = new
-    m_high, m_low = split(new)
-    m_high_out[...] = m_high
-    m_low_out[...] = m_low
-    near = product(faces_high[...], faces_low[...], m_high, m_low)
+    near = jnp.zeros((2 * FSLOT, COLS), f32)
+    for number in range(CHUNKS):
+        part = chunk(number)
+        lowest = jnp.concatenate([floor[part, :].astype(f32)] * (COLS // FSLOT), axis=1)
+        new = jnp.maximum(m[part, :] - gradient[part, :] * rate, lowest)
+        m_out[part, :] = new
+        m_high, m_low = split(new)
+        m_high_out[part, :] = m_high
+        m_low_out[part, :] = m_low
+        near += product(faces_high[:, part], faces_low[:, part], m_high, m_low)
     near_x_out[...] = near[:FSLOT]
     near_y_out[...] = near[FSLOT:]
 

time: 151 us -> 151 us (level)
  no operation moved by 1% of the time
where the time goes in v6:
time: 151 us; the launch traced here: 150 us
  blocking collectives  97.7 us (65%)
  starting transfers between devices  31.5 us (21%)
  Pallas kernels  10.7 us (7%)
  waiting for transfers between devices  10.1 us (7%)
    all_to_all x6, blocking collectives, from_everyone(): return lax.all_to_all(copies, axis, split_axis=0, concat_axis=0, tiled=True)  97.7 us
    ppermute x6, starting transfers between devices, swapped(): return lax.ppermute(block, axis, route)  23.2 us
    pallas_call x13, Pallas kernels, call(): pl.pallas_call(kernel, out_shape=tuple((shape for shape, _ in outs)), in_...  10.7 us
    ppermute x6, waiting for transfers between devices, swapped_by_core(): return lax.ppermute(block, ('c', 'y', 'x'), route)  9.17 us
    ppermute x6, starting transfers between devices, swapped_by_core(): return lax.ppermute(block, ('c', 'y', 'x'), route)  8.31 us
  transfers between devices with their start and end apart: 12, of which 4 were waited for; matrix products, arithmetic and copies ran while one was open for 0% of the time, Pallas kernels for 2%

profile of v6, /device:TPU:1, one launch (start us, length us, event | category | flops | bytes accessed | tf_op | source)
XLA Modules:
  0.0 150.3 jit_solution(2092919273869027660)
XLA Ops:
  0.0 3.8 %shard_map.73 = (bf16[768,768]{1,0:T(8,128)(2,1)S(1)}, bf16[768,768]{1,0:T(8,128)(2,1)S(1)}, bf16[256,768]{1,0:T(8,128)(2,1)S(1)}, bf16[256,768]{1,0:T(8,128)(2,...) custom-call(s32[16,32]{1,0:T(8,128)} %bitcast.11, ...), custom_call_target="tpu_custom_call" | custom-call | tf_op jit(solution)/shard_map/pallas_call | solution.py:186
  3.8 8.7 %collective-permute-start.1 = (f32[128,256]{1,0:T(8,128)S(1)}, f32[128,256]{1,0:T(8,128)S(1)}, u32[]{:S(2)}, u32[]{:S(2)}) collective-permute-start(f32[128,256]{1,0:T(8,128)S(1)} %get-tuple-element.39), channel_id=1, source_target_pairs={{0,16},{16,0},{32,48},{48,32},{64,80},{80,64},{96,112},{112,96},{1... | collective-permute-start | bytes 393224 | tf_op jit(solution)/shard_map/ppermute | solution.py:200
  12.5 1.9 %collective-permute-start = (f32[128,256]{1,0:T(8,128)S(1)}, f32[128,256]{1,0:T(8,128)S(1)}, u32[]{:S(2)}, u32[]{:S(2)}) collective-permute-start(f32[128,256]{1,0:T(8,128)S(1)} %get-tuple-element.39), channel_id=1, source_target_pairs={{16,32},{32,16},{48,64},{64,48},{80,96},{96,80},{112,128},{128,112... | collective-permute-start | bytes 393224 | tf_op jit(solution)/shard_map/ppermute | solution.py:200
  14.4 1.9 %collective-permute-start.3 = (f32[128,256]{1,0:T(8,128)S(1)}, f32[128,256]{1,0:T(8,128)S(1)}, u32[]{:S(2)}, u32[]{:S(2)}) collective-permute-start(f32[128,256]{1,0:T(8,128)S(1)} %get-tuple-element.40), channel_id=1, source_target_pairs={{1,2},{2,1},{3,4},{4,3},{5,6},{6,5},{7,8},{8,7},{9,10},{10,9},{11,... | collective-permute-start | bytes 393224 | tf_op jit(solution)/shard_map/ppermute | solution.py:210
  17.1 1.1 shard_map.74.local
  18.2 0.9 collective-permute-done.outer
  19.1 2.6 %collective-permute-done.3.above = f32[128,256]{1,0:T(8,128)S(1)} collective-permute-done((f32[128,256]{1,0:T(8,128)S(1)}, f32[128,256]{1,0:T(8,128)S(1)}, u32[]{:S(2)}, u32[]{:S(2)}) %collective-permute-start.3) | collective-permute-done | bytes 131104 | tf_op jit(solution)/shard_map/ppermute | solution.py:210
  22.1 13.0 %all_to_all.30.everything = f32[32,1,256]{2,1,0:T(1,128)S(1)} all-to-all(f32[32,1,256]{2,1,0:T(1,128)S(1)} %get-tuple-element.41), channel_id=1, replica_groups=mesh['z1'=4,'z0'=4,'c'=2,'y'=4,'x'=4] {'c','y','x'}, dimensions={0} | all-to-all | bytes 65536 | tf_op jit(solution)/shard_map/all_to_all | solution.py:214
  35.1 25.1 %all_to_all.31.everything = f32[16,1,256]{2,1,0:T(1,128)S(1)} all-to-all(f32[16,1,256]{2,1,0:T(1,128)S(1)} %shard_map.76), channel_id=1, replica_groups=mesh['z1'=4,'z0'=4,'c'=2,'y'=4,'x'=4] {'z0','z1'}, dimensions={0} | all-to-all | bytes 32768 | tf_op jit(solution)/shard_map/all_to_all | solution.py:214
  60.8 4.0 %collective-permute-start.5 = (f32[128,256]{1,0:T(8,128)S(1)}, f32[128,256]{1,0:T(8,128)S(1)}, u32[]{:S(2)}, u32[]{:S(2)}) collective-permute-start(f32[128,256]{1,0:T(8,128)S(1)} %get-tuple-element.49), channel_id=1, source_target_pairs={{0,16},{16,0},{32,48},{48,32},{64,80},{80,64},{96,112},{112,96},{1... | collective-permute-start | bytes 393224 | tf_op jit(solution)/shard_map/ppermute | solution.py:200
  64.8 2.3 %collective-permute-start.4 = (f32[128,256]{1,0:T(8,128)S(1)}, f32[128,256]{1,0:T(8,128)S(1)}, u32[]{:S(2)}, u32[]{:S(2)}) collective-permute-start(f32[128,256]{1,0:T(8,128)S(1)} %get-tuple-element.49), channel_id=1, source_target_pairs={{16,32},{32,16},{48,64},{64,48},{80,96},{96,80},{112,128},{128,112... | collective-permute-start | bytes 393224 | tf_op jit(solution)/shard_map/ppermute | solution.py:200
  67.1 2.2 %collective-permute-start.7 = (f32[128,256]{1,0:T(8,128)S(1)}, f32[128,256]{1,0:T(8,128)S(1)}, u32[]{:S(2)}, u32[]{:S(2)}) collective-permute-start(f32[128,256]{1,0:T(8,128)S(1)} %get-tuple-element.50), channel_id=1, source_target_pairs={{1,2},{2,1},{3,4},{4,3},{5,6},{6,5},{7,8},{8,7},{9,10},{10,9},{11,... | collective-permute-start | bytes 393224 | tf_op jit(solution)/shard_map/ppermute | solution.py:210
  70.0 1.1 shard_map.78.local
  71.1 3.3 %collective-permute-done.7.above = f32[128,256]{1,0:T(8,128)S(1)} collective-permute-done((f32[128,256]{1,0:T(8,128)S(1)}, f32[128,256]{1,0:T(8,128)S(1)}, u32[]{:S(2)}, u32[]{:S(2)}) %collective-permute-start.7) | collective-permute-done | bytes 131104 | tf_op jit(solution)/shard_map/ppermute | solution.py:210
  74.8 12.8 %all_to_all.32.everything = f32[32,1,256]{2,1,0:T(1,128)S(1)} all-to-all(f32[32,1,256]{2,1,0:T(1,128)S(1)} %get-tuple-element.51), channel_id=1, replica_groups=mesh['z1'=4,'z0'=4,'c'=2,'y'=4,'x'=4] {'c','y','x'}, dimensions={0} | all-to-all | bytes 65536 | tf_op jit(solution)/shard_map/all_to_all | solution.py:214
  87.6 17.1 %all_to_all.33.everything = f32[16,1,256]{2,1,0:T(1,128)S(1)} all-to-all(f32[16,1,256]{2,1,0:T(1,128)S(1)} %shard_map.80), channel_id=1, replica_groups=mesh['z1'=4,'z0'=4,'c'=2,'y'=4,'x'=4] {'z0','z1'}, dimensions={0} | all-to-all | bytes 32768 | tf_op jit(solution)/shard_map/all_to_all | solution.py:214
  105.3 4.0 %collective-permute-start.9 = (f32[128,256]{1,0:T(8,128)S(1)}, f32[128,256]{1,0:T(8,128)S(1)}, u32[]{:S(2)}, u32[]{:S(2)}) collective-permute-start(f32[128,256]{1,0:T(8,128)S(1)} %get-tuple-element.56), channel_id=1, source_target_pairs={{0,16},{16,0},{32,48},{48,32},{64,80},{80,64},{96,112},{112,96},{1... | collective-permute-start | bytes 393224 | tf_op jit(solution)/shard_map/ppermute | solution.py:200
  109.3 2.3 %collective-permute-start.8 = (f32[128,256]{1,0:T(8,128)S(1)}, f32[128,256]{1,0:T(8,128)S(1)}, u32[]{:S(2)}, u32[]{:S(2)}) collective-permute-start(f32[128,256]{1,0:T(8,128)S(1)} %get-tuple-element.56), channel_id=1, source_target_pairs={{16,32},{32,16},{48,64},{64,48},{80,96},{96,80},{112,128},{128,112... | collective-permute-start | bytes 393224 | tf_op jit(solution)/shard_map/ppermute | solution.py:200
  111.6 2.2 %collective-permute-start.11 = (f32[128,256]{1,0:T(8,128)S(1)}, f32[128,256]{1,0:T(8,128)S(1)}, u32[]{:S(2)}, u32[]{:S(2)}) collective-permute-start(f32[128,256]{1,0:T(8,128)S(1)} %get-tuple-element.57), channel_id=1, source_target_pairs={{1,2},{2,1},{3,4},{4,3},{5,6},{6,5},{7,8},{8,7},{9,10},{10,9},{11,... | collective-permute-start | bytes 393224 | tf_op jit(solution)/shard_map/ppermute | solution.py:210
  114.5 1.1 shard_map.82.local
  115.6 3.3 %collective-permute-done.11.above = f32[128,256]{1,0:T(8,128)S(1)} collective-permute-done((f32[128,256]{1,0:T(8,128)S(1)}, f32[128,256]{1,0:T(8,128)S(1)}, u32[]{:S(2)}, u32[]{:S(2)}) %collective-permute-start.11) | collective-permute-done | bytes 131104 | tf_op jit(solution)/shard_map/ppermute | solution.py:210
  119.3 12.8 %all_to_all.34.everything = f32[32,1,256]{2,1,0:T(1,128)S(1)} all-to-all(f32[32,1,256]{2,1,0:T(1,128)S(1)} %get-tuple-element.58), channel_id=1, replica_groups=mesh['z1'=4,'z0'=4,'c'=2,'y'=4,'x'=4] {'c','y','x'}, dimensions={0} | all-to-all | bytes 65536 | tf_op jit(solution)/shard_map/all_to_all | solution.py:214
  132.1 17.1 %all_to_all.35.everything = f32[16,1,256]{2,1,0:T(1,128)S(1)} all-to-all(f32[16,1,256]{2,1,0:T(1,128)S(1)} %shard_map.84), channel_id=1, replica_groups=mesh['z1'=4,'z0'=4,'c'=2,'y'=4,'x'=4] {'z0','z1'}, dimensions={0} | all-to-all | bytes 32768 | tf_op jit(solution)/shard_map/all_to_all | solution.py:214
  149.2 1.1 shard_map.85
  (19 shorter events, 4.6 us)
Async XLA Ops:
  3.8 14.4 %collective-permute-start.1 = (f32[128,256]{1,0:T(8,128)S(1)}, f32[128,256]{1,0:T(8,128)S(1)}, u32[]{:S(2)}, u32[]{:S(2)}) collective-permute-start(f32[128,256]{1,0:T(8,128)S(1)} %get-tuple-element.39), channel_id=1, source_target_pairs={{0,16},{16,0},{32,48},{48,32},{64,80},{80,64},{96,112},{112,96},{1... | collective-permute-start | bytes 393224 | tf_op jit(solution)/shard_map/ppermute | solution.py:200
  12.5 6.6 %collective-permute-start = (f32[128,256]{1,0:T(8,128)S(1)}, f32[128,256]{1,0:T(8,128)S(1)}, u32[]{:S(2)}, u32[]{:S(2)}) collective-permute-start(f32[128,256]{1,0:T(8,128)S(1)} %get-tuple-element.39), channel_id=1, source_target_pairs={{16,32},{32,16},{48,64},{64,48},{80,96},{96,80},{112,128},{128,112... | collective-permute-start | bytes 393224 | tf_op jit(solution)/shard_map/ppermute | solution.py:200
  14.4 7.2 %collective-permute-start.3 = (f32[128,256]{1,0:T(8,128)S(1)}, f32[128,256]{1,0:T(8,128)S(1)}, u32[]{:S(2)}, u32[]{:S(2)}) collective-permute-start(f32[128,256]{1,0:T(8,128)S(1)} %get-tuple-element.40), channel_id=1, source_target_pairs={{1,2},{2,1},{3,4},{4,3},{5,6},{6,5},{7,8},{8,7},{9,10},{10,9},{11,... | collective-permute-start | bytes 393224 | tf_op jit(solution)/shard_map/ppermute | solution.py:210
  16.4 5.3 %collective-permute-start.2 = (f32[128,256]{1,0:T(8,128)S(1)}, f32[128,256]{1,0:T(8,128)S(1)}, u32[]{:S(2)}, u32[]{:S(2)}) collective-permute-start(f32[128,256]{1,0:T(8,128)S(1)} %get-tuple-element.40), channel_id=1, source_target_pairs={{0,1},{1,0},{2,3},{3,2},{4,5},{5,4},{6,7},{7,6},{8,9},{9,8},{10,11... | collective-permute-start | bytes 393224 | tf_op jit(solution)/shard_map/ppermute | solution.py:210
  60.8 10.3 %collective-permute-start.5 = (f32[128,256]{1,0:T(8,128)S(1)}, f32[128,256]{1,0:T(8,128)S(1)}, u32[]{:S(2)}, u32[]{:S(2)}) collective-permute-start(f32[128,256]{1,0:T(8,128)S(1)} %get-tuple-element.49), channel_id=1, source_target_pairs={{0,16},{16,0},{32,48},{48,32},{64,80},{80,64},{96,112},{112,96},{1... | collective-permute-start | bytes 393224 | tf_op jit(solution)/shard_map/ppermute | solution.py:200
  64.8 6.3 %collective-permute-start.4 = (f32[128,256]{1,0:T(8,128)S(1)}, f32[128,256]{1,0:T(8,128)S(1)}, u32[]{:S(2)}, u32[]{:S(2)}) collective-permute-start(f32[128,256]{1,0:T(8,128)S(1)} %get-tuple-element.49), channel_id=1, source_target_pairs={{16,32},{32,16},{48,64},{64,48},{80,96},{96,80},{112,128},{128,112... | collective-permute-start | bytes 393224 | tf_op jit(solution)/shard_map/ppermute | solution.py:200
  67.1 7.3 %collective-permute-start.7 = (f32[128,256]{1,0:T(8,128)S(1)}, f32[128,256]{1,0:T(8,128)S(1)}, u32[]{:S(2)}, u32[]{:S(2)}) collective-permute-start(f32[128,256]{1,0:T(8,128)S(1)} %get-tuple-element.50), channel_id=1, source_target_pairs={{1,2},{2,1},{3,4},{4,3},{5,6},{6,5},{7,8},{8,7},{9,10},{10,9},{11,... | collective-permute-start | bytes 393224 | tf_op jit(solution)/shard_map/ppermute | solution.py:210
  69.3 5.1 %collective-permute-start.6 = (f32[128,256]{1,0:T(8,128)S(1)}, f32[128,256]{1,0:T(8,128)S(1)}, u32[]{:S(2)}, u32[]{:S(2)}) collective-permute-start(f32[128,256]{1,0:T(8,128)S(1)} %get-tuple-element.50), channel_id=1, source_target_pairs={{0,1},{1,0},{2,3},{3,2},{4,5},{5,4},{6,7},{7,6},{8,9},{9,8},{10,11... | collective-permute-start | bytes 393224 | tf_op jit(solution)/shard_map/ppermute | solution.py:210
  105.3 10.3 %collective-permute-start.9 = (f32[128,256]{1,0:T(8,128)S(1)}, f32[128,256]{1,0:T(8,128)S(1)}, u32[]{:S(2)}, u32[]{:S(2)}) collective-permute-start(f32[128,256]{1,0:T(8,128)S(1)} %get-tuple-element.56), channel_id=1, source_target_pairs={{0,16},{16,0},{32,48},{48,32},{64,80},{80,64},{96,112},{112,96},{1... | collective-permute-start | bytes 393224 | tf_op jit(solution)/shard_map/ppermute | solution.py:200
  109.3 6.3 %collective-permute-start.8 = (f32[128,256]{1,0:T(8,128)S(1)}, f32[128,256]{1,0:T(8,128)S(1)}, u32[]{:S(2)}, u32[]{:S(2)}) collective-permute-start(f32[128,256]{1,0:T(8,128)S(1)} %get-tuple-element.56), channel_id=1, source_target_pairs={{16,32},{32,16},{48,64},{64,48},{80,96},{96,80},{112,128},{128,112... | collective-permute-start | bytes 393224 | tf_op jit(solution)/shard_map/ppermute | solution.py:200
  111.6 7.3 %collective-permute-start.11 = (f32[128,256]{1,0:T(8,128)S(1)}, f32[128,256]{1,0:T(8,128)S(1)}, u32[]{:S(2)}, u32[]{:S(2)}) collective-permute-start(f32[128,256]{1,0:T(8,128)S(1)} %get-tuple-element.57), channel_id=1, source_target_pairs={{1,2},{2,1},{3,4},{4,3},{5,6},{6,5},{7,8},{8,7},{9,10},{10,9},{11,... | collective-permute-start | bytes 393224 | tf_op jit(solution)/shard_map/ppermute | solution.py:210
  113.8 5.1 %collective-permute-start.10 = (f32[128,256]{1,0:T(8,128)S(1)}, f32[128,256]{1,0:T(8,128)S(1)}, u32[]{:S(2)}, u32[]{:S(2)}) collective-permute-start(f32[128,256]{1,0:T(8,128)S(1)} %get-tuple-element.57), channel_id=1, source_target_pairs={{0,1},{1,0},{2,3},{3,2},{4,5},{5,4},{6,7},{7,6},{8,9},{9,8},{10,11... | collective-permute-start | bytes 393224 | tf_op jit(solution)/shard_map/ppermute | solution.py:210
